TPU v7x, 128 devices: a whole 4x4x4 slice. The times are simulated.
128 devices in a mesh: grp: 2 (over core), dev: 64 (over x, y, z).
Axes of the slice: x: 4, y: 4, z: 4, core: 2. Of those that a mesh axis runs over, the one named last changes fastest.
Arguments:
- residual_in: bfloat16 [2048, 2048], P(('grp', 'dev')), may hold values from -1.5 to 1.5
- queries: bfloat16 [2, 1024, 4096], P(None, 'dev', 'grp'), may hold values from -2.5 to 2.5
- latest_key_value: bfloat16 [2, 1024, 4, 256], P(None, 'dev', 'grp'), may hold values from -2.5 to 2.5
- key_value_cache: bfloat16 [2, 1024, 4, 256, 256], P(None, 'dev', 'grp'), may hold values from -2.5 to 2.5
- cache_len: int32 [2, 1024], P(None, 'dev'), may hold values from 1 to 256, 131072 in all within a row
- out_weight: bfloat16 [4096, 2048], P('grp'), may hold values from -0.09375 to 0.09375
- norm_gain: bfloat16 [2048], replicated, may hold values from 0.099609375 to 1.8984375
- router_weight: bfloat16 [2048, 128], replicated, may hold values from -0.125 to 0.125
- routes: int32 [2048, 8], P(('grp', 'dev')), may hold values from 0 to 127, all different within a row; in each aligned block of 16 rows (0 to 15, 16 to 31, ...) at most 2 rows name the same one
- expert_gate_up: bfloat16 [128, 2048, 1536], P(('grp', 'dev')), may hold values from -0.125 to 0.125
- expert_down: bfloat16 [128, 768, 2048], P(('grp', 'dev')), may hold values from -0.21875 to 0.21875
Outputs:
- layer_out: bfloat16 [2048, 2048], P(('grp', 'dev'))
Inputs may be any that keep to these rules, and one draw needn't show every extreme that they name: Each row of cache_len of 1024 entries sums to 131072, and its largest entry is exactly 256. `routes`: the 8 experts of a row are distinct; in each aligned block of 16 rows (the rows of one device) no expert is named by more than 2 rows, a bound that some block reaches.
All inputs are finite; a program needn't handle non-finite values. No bound on the sum of `cache_len` on one device may be relied on, other than what follows from the above.
Results may differ from a plain program's by a relative error of at most 0.017.
Values may be sent and summed in bfloat16 or wider, within the bound.
No kernel may reach another device: no remote copies, remote signals or barrier semaphores. Data moves between devices by JAX's collectives and lax.ppermute only.
A program may use at most 128 MiB of HBM per device.

v0:
```python
import math

import jax
import jax.numpy as jnp
from jax import lax
from jax.sharding import PartitionSpec as P

HEAD_SIZE = 128
FF = 768


def per_device(
    residual_in,
    queries,
    latest_key_value,
    key_value_cache,
    cache_len,
    out_weight,
    norm_gain,
    router_weight,
    routes,
    expert_gate_up,
    expert_down,
):
    halves = queries.shape[0]
    tokens = queries.shape[1]
    kv_heads = key_value_cache.shape[2]
    positions = key_value_cache.shape[3]
    q_heads = queries.shape[2] // HEAD_SIZE
    query_group = q_heads // kv_heads
    width = residual_in.shape[1]
    scale = 1.0 / math.sqrt(HEAD_SIZE)
    query_vector = queries.reshape(halves, tokens, kv_heads, query_group, HEAD_SIZE)
    scores = (
        jnp.einsum(
            "hrkgd,hrksd->hrkgs",
            query_vector,
            key_value_cache[..., :HEAD_SIZE],
            preferred_element_type=jnp.float32,
        )
        * scale
    )
    own_score = (
        jnp.einsum(
            "hrkgd,hrkd->hrkg",
            query_vector,
            latest_key_value[..., :HEAD_SIZE],
            preferred_element_type=jnp.float32,
        )
        * scale
    )
    visible = (
        jnp.arange(positions, dtype=jnp.int32)[None, None, None, None, :]
        < cache_len[:, :, None, None, None]
    )
    raised = jnp.where(visible, jnp.exp(scores), 0.0)
    own_raised = jnp.exp(own_score)
    totals = jnp.sum(raised, axis=-1) + own_raised
    weights = (raised / totals[..., None]).astype(jnp.bfloat16)
    own_weight = (own_raised / totals).astype(jnp.bfloat16)
    mixed = jnp.einsum(
        "hrkgs,hrksd->hrkgd",
        weights,
        key_value_cache[..., HEAD_SIZE:],
        preferred_element_type=jnp.float32,
    )
    mixed = (
        mixed
        + own_weight.astype(jnp.float32)[..., None]
        * latest_key_value[..., HEAD_SIZE:].astype(jnp.float32)[:, :, :, None, :]
    )
    attended = mixed.astype(jnp.bfloat16).reshape(halves * tokens, q_heads * HEAD_SIZE)
    partial_value = jnp.dot(attended, out_weight, preferred_element_type=jnp.float32).reshape(
        halves, tokens, width
    )
    summed = lax.psum(partial_value, "grp")
    projected = lax.dynamic_index_in_dim(summed, lax.axis_index("grp"), 0, keepdims=False)
    hidden = residual_in.astype(jnp.float32) + projected
    meansq = jnp.mean(hidden * hidden, axis=-1, keepdims=True)
    normed = (hidden * lax.rsqrt(meansq + 1e-06) * norm_gain.astype(jnp.float32)).astype(
        jnp.bfloat16
    )
    logits = jnp.dot(normed, router_weight, preferred_element_type=jnp.float32)
    picked = jnp.exp(jnp.take_along_axis(logits, routes, axis=1))
    gates = picked / jnp.sum(picked, axis=1, keepdims=True)
    batch_rows = routes.shape[0]
    topk = routes.shape[1]
    experts_all = router_weight.shape[1]
    capacity = max(2, 2 * batch_rows * topk // experts_all)
    flat_routes = routes.reshape(batch_rows * topk)
    onehot = (flat_routes[:, None] == jnp.arange(experts_all, dtype=jnp.int32)[None, :]).astype(
        jnp.int32
    )
    ranks = jnp.sum(onehot * (jnp.cumsum(onehot, axis=0) - 1), axis=1)
    target = flat_routes * capacity + ranks
    selector = (
        target[None, :] == jnp.arange(experts_all * capacity, dtype=jnp.int32)[:, None]
    ).astype(jnp.int32)
    selector = jnp.sum(selector.reshape(experts_all * capacity, batch_rows, topk), axis=2).astype(
        jnp.bfloat16
    )
    outgoing = jnp.dot(selector, normed, preferred_element_type=jnp.float32).astype(jnp.bfloat16)
    outgoing = outgoing.reshape(experts_all, capacity, width)
    received = lax.all_to_all(outgoing, ("grp", "dev"), split_axis=0, concat_axis=0, tiled=True)
    count = received.shape[0] * received.shape[1]
    gate_up = jnp.dot(
        received.reshape(count, width), expert_gate_up[0], preferred_element_type=jnp.float32
    )
    active = (jax.nn.silu(gate_up[:, :FF]) * gate_up[:, FF:]).astype(jnp.bfloat16)
    result = jnp.dot(active, expert_down[0], preferred_element_type=jnp.float32).astype(
        jnp.bfloat16
    )
    returned = lax.all_to_all(
        result.reshape(received.shape), ("grp", "dev"), split_axis=0, concat_axis=0, tiled=True
    )
    table = returned.reshape(experts_all * capacity, width)
    gathered = table[target].reshape(batch_rows, topk, width).astype(jnp.float32)
    combined = jnp.sum(gates[:, :, None] * gathered, axis=1)
    return (hidden + combined).astype(jnp.bfloat16)


def solution(mesh):
    placed = (
        P(("grp", "dev"), None),
        P(None, "dev", "grp"),
        P(None, "dev", "grp", None),
        P(None, "dev", "grp", None, None),
        P(None, "dev"),
        P("grp", None),
        P(),
        P(),
        P(("grp", "dev"), None),
        P(("grp", "dev"), None, None),
        P(("grp", "dev"), None, None),
    )
    return jax.shard_map(
        per_device, mesh=mesh, in_specs=placed, out_specs=P(("grp", "dev"), None), check_vma=False
    )
```

profile of v0, /device:TPU:0, one launch (start us, length us, event | category | flops | bytes accessed | tf_op | source)
XLA Modules:
  0.0 132.5 jit_solution(18427662515495649888)
XLA Ops:
  6.5 0.0 copy-start
  6.5 0.0 all-reduce.2.cloned.1.call-start
  6.5 0.9 iota_compare_fusion.2
  7.4 0.8 slice_convert_fusion
  8.3 0.9 copy.29
  9.2 0.2 fusion.34
  9.4 3.5 %fusion.43 = (f32[2,16,2,8]{3,2,1,0:T(2,128)S(1)}, f32[2,16,2,8,256]{4,3,2,1,0:T(8,128)S(1)}) fusion(bf16[2,16,2,8,128]{4,3,2,1,0:T(8,128)(2,1)S(1)} %bitcast.50, bf16[2,16,2,256,256]{4,3,2,1,0:T(8,128)(2,1)} %param.14, pred[2,16,256]{2,1,0:T(8,128)(4,1)S(1)} %iota_compare_fusion.2), kind=kOutput, calls=%fused_computation.58 | convolution fusion | flops 33947136 | bytes 4859904 | tf_op jit(solution)/shard_map/hrkgd,hrksd->hrkgs/dot_general | solution.py:35
  12.9 2.9 %fusion.25 = bf16[2,16,2,8,128]{4,3,2,1,0:T(8,128)(2,1)S(1)} fusion(bf16[2,16,2,256,256]{4,3,2,1,0:T(8,128)(2,1)} %param.14, f32[2,16,2,8,256]{4,3,2,1,0:T(8,128)S(1)} %get-tuple-element.12, f32[2,16,2,8]{3,2,1,0:T(2,128)S(1)} %get-tuple-element.6, f32[2,16,2,128]{3,2,1,0:T(2,128)S(1)} %get-tuple-element.7, f32[2,16,2,8]{3,2,1,0:T(2,128)S(1)} %get-tuple-element.5), kind=kOutput, calls=%fused_computation.18 | convolution fusion | flops 34013184 | bytes 4886528 | tf_op jit(solution)/shard_map/hrkgs,hrksd->hrkgd/dot_general | solution.py:61
  15.9 0.1 dot_general.29
  15.9 0.0 copy-start.3
  16.0 0.0 copy-start.4
  16.0 0.0 copy-start.2
  16.0 5.7 %fusion = f32[2,16,2048]{2,1,0:T(8,128)} fusion(bf16[2,16,2048]{2,1,0:T(8,128)(2,1)S(1)} %dot_general.29, bf16[2048,2048]{1,0:T(8,128)(2,1)} %param.16), kind=kOutput, calls=%fused_computation.2 | convolution fusion | flops 268435456 | bytes 8781824 | tf_op jit(solution)/shard_map/dot_general | solution.py:73
  21.6 0.0 all-reduce.2.cloned.1.call-update
  21.7 0.0 copy-done.3
  21.7 0.1 copy.25
  21.7 0.1 eq.29
  21.8 0.0 copy-done.4
  21.9 0.1 fusion.33
  21.9 0.2 reduce_window_sum.11
  22.1 0.2 select_reduce_fusion
  22.3 0.1 reduce_sum.62
  22.4 0.1 convert_reduce_fusion
  22.5 25.6 %all-reduce.2.cloned.1.call-done = f32[2,16,2048]{2,1,0:T(8,128)} async-done(((f32[2,16,2048]{2,1,0:T(8,128)}), f32[2,16,2048]{2,1,0:T(8,128)}) %all-reduce.2.cloned.1.call-update) | async-done | bytes 262160 | tf_op jit(solution)/shard_map/psum | solution.py:76
  48.1 0.0 copy-done.2
  48.1 1.0 multiply_reduce_fusion
  49.1 1.0 multiply_convert_fusion
  50.1 1.5 %convolution_convert_fusion = bf16[256,2048]{1,0:T(8,128)(2,1)} fusion(bf16[16,2048]{1,0:T(8,128)(2,1)S(1)} %multiply_convert_fusion, s32[256,16]{0,1:T(8,128)S(1)} %convert_reduce_fusion), kind=kOutput, calls=%fused_computation.13 | convolution fusion | flops 17305600 | bytes 1130496 | tf_op jit(solution)/shard_map/dot_general | solution.py:102
  51.6 2.5 %reshape.112 = bf16[128,2,2048]{2,1,0:T(2,128)(2,1)} reshape(bf16[256,2048]{1,0:T(8,128)(2,1)} %convolution_convert_fusion) | data formatting | bytes 2097152 | tf_op jit(solution)/shard_map/reshape | solution.py:103
  54.2 28.3 %all_to_all.10 = bf16[128,2,2048]{2,1,0:T(2,128)(2,1)} all-to-all(bf16[128,2,2048]{2,1,0:T(2,128)(2,1)} %reshape.112), channel_id=1, replica_groups=mesh['grp'=2,'dev'=64] {'grp','dev'}, dimensions={0} | all-to-all | bytes 2097152 | tf_op jit(solution)/shard_map/all_to_all | solution.py:104
  82.4 2.3 %reshape.113 = bf16[256,2048]{1,0:T(8,128)(2,1)} reshape(bf16[128,2,2048]{2,1,0:T(2,128)(2,1)} %all_to_all.10) | data formatting | bytes 2097152 | tf_op jit(solution)/shard_map/reshape | solution.py:107
  84.7 4.9 %fusion.2 = f32[256,1536]{1,0:T(8,128)S(1)} fusion(bf16[256,2048]{1,0:T(8,128)(2,1)} %reshape.113, bf16[1,2048,1536]{2,1,0:T(8,128)(2,1)} %param.20), kind=kOutput, calls=%fused_computation.4 | convolution fusion | flops 1610612736 | bytes 8912896 | tf_op jit(solution)/shard_map/dot_general | solution.py:106
  89.6 0.0 copy-done
  89.6 2.0 %fusion.10 = bf16[256,2048]{1,0:T(8,128)(2,1)} fusion(bf16[1,768,2048]{2,1,0:T(8,128)(2,1)S(1)} %copy-done, f32[256,1536]{1,0:T(8,128)S(1)} %fusion.2), kind=kOutput, calls=%fused_computation.12 | convolution fusion | flops 807010304 | bytes 5767168 | tf_op jit(solution)/shard_map/dot_general | solution.py:110
  91.7 2.5 %reshape.114 = bf16[128,2,2048]{2,1,0:T(2,128)(2,1)} reshape(bf16[256,2048]{1,0:T(8,128)(2,1)} %fusion.10) | data formatting | bytes 2097152 | tf_op jit(solution)/shard_map/reshape | solution.py:114
  94.2 5.8 %all-to-all-start.1 = ((bf16[128,2,2048]{2,1,0:T(2,128)(2,1)}), bf16[128,2,2048]{2,1,0:T(2,128)(2,1)}, u32[]{:S(2)}, u32[]{:S(2)}) async-start(bf16[128,2,2048]{2,1,0:T(2,128)(2,1)} %reshape.114), calls=%async_computation.1 | async-start | bytes 2097152 | tf_op jit(solution)/shard_map/all_to_all | solution.py:113
  100.0 0.1 copy.22
  100.1 0.1 reshape.125
  100.2 0.1 mul.100
  100.3 1.2 fusion.44
  101.5 1.3 gather_fusion.1
  102.8 0.0 copy-start.1
  102.8 0.1 reshape.128
  102.9 0.1 copy.23
  103.0 0.1 copy.24
  103.0 14.6 %all-to-all-done.1 = bf16[128,2,2048]{2,1,0:T(2,128)(2,1)} async-done(((bf16[128,2,2048]{2,1,0:T(2,128)(2,1)}), bf16[128,2,2048]{2,1,0:T(2,128)(2,1)}, u32[]{:S(2)}, u32[]{:S(2)}) %all-to-all-start.1) | async-done | bytes 1048608 | tf_op jit(solution)/shard_map/all_to_all | solution.py:113
  117.7 2.3 %reshape.115 = bf16[256,2048]{1,0:T(8,128)(2,1)} reshape(bf16[128,2,2048]{2,1,0:T(2,128)(2,1)} %all-to-all-done.1) | data formatting | bytes 2097152 | tf_op jit(solution)/shard_map/reshape | solution.py:116
  119.9 3.6 %gather_fusion = bf16[128,2048]{1,0:T(8,128)(2,1)} fusion(bf16[256,2048]{1,0:T(8,128)(2,1)} %reshape.115, s32[1024]{0:T(1024)S(1)} %pad_clamp_fusion), kind=kCustom, calls=%fused_computation | custom fusion | bytes 1049088 | tf_op jit(solution)/shard_map/gather | solution.py:117
  123.5 1.5 %fusion.28 = f32[16,2048]{1,0:T(8,128)S(1)} fusion(bf16[128,2048]{1,0:T(8,128)(2,1)} %gather_fusion, f32[16,8]{1,0:T(8,128)S(1)} %copy.24), kind=kLoop, calls=%fused_computation.20 | loop fusion | flops 753664 | bytes 655872 | tf_op jit(solution)/shard_map/reduce_sum | solution.py:118
  125.0 0.0 copy-done.1
  125.0 0.7 add_convert_fusion
  (9 shorter events, 0.1 us)
Async XLA Ops:
  6.5 83.1 %copy-start = (bf16[1,768,2048]{2,1,0:T(8,128)(2,1)S(1)}, bf16[1,768,2048]{2,1,0:T(8,128)(2,1)}, u32[]{:S(2)}) copy-start(bf16[1,768,2048]{2,1,0:T(8,128)(2,1)} %param.21) | copy-start | bytes 9437188
  6.5 41.5 %all-reduce.2.cloned.1.call-start = ((), (), s32[]{:S(2)}) async-start(), calls=%async_computation.2 | async-start | bytes 524288 | tf_op jit(solution)/shard_map/psum | solution.py:76
  15.9 5.7 %copy-start.3 = (s32[16,8]{0,1:T(8,128)S(1)}, s32[16,8]{0,1:T(8,128)}, u32[]{:S(2)}) copy-start(s32[16,8]{0,1:T(8,128)} %param.19) | copy-start | bytes 1540
  16.0 5.9 %copy-start.4 = (bf16[2048]{0:T(1024)(128)(2,1)S(1)}, bf16[2048]{0:T(1024)(128)(2,1)}, u32[]{:S(2)}) copy-start(bf16[2048]{0:T(1024)(128)(2,1)} %param.17) | copy-start | bytes 12292
  16.0 32.1 %copy-start.2 = (bf16[16,2048]{1,0:T(8,128)(2,1)S(1)}, bf16[16,2048]{1,0:T(8,128)(2,1)}, u32[]{:S(2)}) copy-start(bf16[16,2048]{1,0:T(8,128)(2,1)} %param.11) | copy-start | bytes 196612
  94.2 23.5 %all-to-all-start.1 = ((bf16[128,2,2048]{2,1,0:T(2,128)(2,1)}), bf16[128,2,2048]{2,1,0:T(2,128)(2,1)}, u32[]{:S(2)}, u32[]{:S(2)}) async-start(bf16[128,2,2048]{2,1,0:T(2,128)(2,1)} %reshape.114), calls=%async_computation.1 | async-start | bytes 2097152 | tf_op jit(solution)/shard_map/all_to_all | solution.py:113
  102.8 22.3 %copy-start.1 = (f32[2,16,2048]{2,1,0:T(8,128)S(1)}, f32[2,16,2048]{2,1,0:T(8,128)}, u32[]{:S(2)}) copy-start(f32[2,16,2048]{2,1,0:T(8,128)} %all-reduce.2.cloned.1.call-done) | copy-start | bytes 786436
Sparse Core Ops, SparseCore 0:
  21.8 26.2 all-reduce.1
where the time goes:
time: 133 us
  waiting for transfers between devices  40.2 us (30%)
  blocking collectives  28.3 us (21%)
  matrix products  21.9 us (16%)
  local copies, waits for them, and re-layouts  16.2 us (12%)
  between operations  13.6 us (10%)
  other arithmetic  6.56 us (5%)
  starting transfers between devices  5.78 us (4%)
    all_to_all x1, blocking collectives, per_device(): lax.all_to_all(outgoing, ('grp', 'dev'), split_axis=0, concat_axis=0, til...  28.3 us
    psum x1, waiting for transfers between devices, per_device(): summed = lax.psum(partial_value, 'grp')  25.6 us
    all_to_all x1, waiting for transfers between devices, per_device(): lax.all_to_all(result.reshape(received.shape), ('grp', 'dev'), split_axis...  14.6 us
    all_to_all x1, starting transfers between devices, per_device(): lax.all_to_all(result.reshape(received.shape), ('grp', 'dev'), split_axis...  5.78 us
    dot_general x1, matrix products, per_device(): jnp.dot(attended, out_weight, preferred_element_type=jnp.float32)  5.65 us
    dot_general x1, matrix products, per_device(): jnp.dot(received.reshape(count, width), expert_gate_up[0], preferred_elem...  4.9 us
    gather x1, local copies, waits for them, and re-layouts, per_device(): table[target].reshape(batch_rows, topk, width).astype(jnp.float32)  3.59 us
    dot_general x1, matrix products, per_device(): jnp.einsum('hrkgd,hrksd->hrkgs', query_vector, key_value_cache[..., :HEAD...  3.5 us
  transfers between devices with their start and end apart: 2, of which 2 were waited for; matrix products, arithmetic and copies ran while one was open for 3% of the time, Pallas kernels for 0%

commit v1 on v0

--- a/solution.py
+++ b/solution.py
@@ -73,8 +73,10 @@
     partial_value = jnp.dot(attended, out_weight, preferred_element_type=jnp.float32).reshape(
         halves, tokens, width
     )
-    summed = lax.psum(partial_value, "grp")
-    projected = lax.dynamic_index_in_dim(summed, lax.axis_index("grp"), 0, keepdims=False)
+    half = lax.axis_index("grp")
+    kept = lax.dynamic_index_in_dim(partial_value, half, 0, keepdims=False)
+    passed = lax.dynamic_index_in_dim(partial_value, 1 - half, 0, keepdims=False)
+    projected = kept + lax.ppermute(passed, "grp", [(0, 1), (1, 0)])
     hidden = residual_in.astype(jnp.float32) + projected
     meansq = jnp.mean(hidden * hidden, axis=-1, keepdims=True)
     normed = (hidden * lax.rsqrt(meansq + 1e-06) * norm_gain.astype(jnp.float32)).astype(

time: 133 us -> 95.7 us (0.72)
  waiting for transfers between devices: 40.2 us -> 14.6 us
  between operations: 13.6 us -> 0.22 us
    psum x1 -> x0, waiting for transfers between devices: 25.6 us -> none  [per_device(): summed = lax.psum(partial_value, 'grp')]
  transfers between devices with their start and end apart: 2 -> 2, of which waited for: 2 -> 1; matrix products, arithmetic and copies ran while one was open for 3% -> 5% of each run, Pallas kernels for 0% -> 0%
where the time goes in v1:
time: 95.7 us; the launch traced here: 95 us
  blocking collectives  29.5 us (31%)
  matrix products  21.3 us (22%)
  local copies, waits for them, and re-layouts  16.9 us (18%)
  waiting for transfers between devices  14.6 us (15%)
  other arithmetic  6.87 us (7%)
  starting transfers between devices  5.78 us (6%)
    all_to_all x1, blocking collectives, per_device(): lax.all_to_all(outgoing, ('grp', 'dev'), split_axis=0, concat_axis=0, til...  29.5 us
    all_to_all x1, waiting for transfers between devices, per_device(): lax.all_to_all(result.reshape(received.shape), ('grp', 'dev'), split_axis...  14.6 us
    all_to_all x1, starting transfers between devices, per_device(): lax.all_to_all(result.reshape(received.shape), ('grp', 'dev'), split_axis...  5.78 us
    dot_general x1, matrix products, per_device(): jnp.dot(attended, out_weight, preferred_element_type=jnp.float32)  4.93 us
    dot_general x1, matrix products, per_device(): jnp.dot(received.reshape(count, width), expert_gate_up[0], preferred_elem...  4.9 us
    gather x1, local copies, waits for them, and re-layouts, per_device(): table[target].reshape(batch_rows, topk, width).astype(jnp.float32)  3.59 us
    dot_general x1, matrix products, per_device(): jnp.einsum('hrkgd,hrksd->hrkgs', query_vector, key_value_cache[..., :HEAD...  3.5 us
    dot_general x1, matrix products, per_device(): jnp.einsum('hrkgs,hrksd->hrkgd', weights, key_value_cache[..., HEAD_SIZE:...  2.91 us
  transfers between devices with their start and end apart: 2, of which 1 were waited for; matrix products, arithmetic and copies ran while one was open for 5% of the time, Pallas kernels for 0%

profile of v1, /device:TPU:0, one launch (start us, length us, event | category | flops | bytes accessed | tf_op | source)
XLA Modules:
  0.0 95.0 jit_solution(4651781939947483389)
XLA Ops:
  0.0 0.0 copy-start
  0.0 0.9 iota_compare_fusion.2
  0.9 0.8 slice_convert_fusion
  1.7 0.9 copy.29
  2.7 0.2 fusion.35
  2.9 3.5 %fusion.46 = (f32[2,16,2,8]{3,2,1,0:T(2,128)S(1)}, f32[2,16,2,8,256]{4,3,2,1,0:T(8,128)S(1)}) fusion(bf16[2,16,2,8,128]{4,3,2,1,0:T(8,128)(2,1)S(1)} %bitcast.47, bf16[2,16,2,256,256]{4,3,2,1,0:T(8,128)(2,1)} %param.14, pred[2,16,256]{2,1,0:T(8,128)(4,1)S(1)} %iota_compare_fusion.2), kind=kOutput, calls=%fused_computation.61 | convolution fusion | flops 33947136 | bytes 4859904 | tf_op jit(solution)/shard_map/hrkgd,hrksd->hrkgs/dot_general | solution.py:35
  6.4 2.9 %fusion.25 = bf16[2,16,2,8,128]{4,3,2,1,0:T(8,128)(2,1)S(1)} fusion(bf16[2,16,2,256,256]{4,3,2,1,0:T(8,128)(2,1)} %param.14, f32[2,16,2,8,256]{4,3,2,1,0:T(8,128)S(1)} %get-tuple-element.14, f32[2,16,2,8]{3,2,1,0:T(2,128)S(1)} %get-tuple-element.8, f32[2,16,2,128]{3,2,1,0:T(2,128)S(1)} %get-tuple-element.9, f32[2,16,2,8]{3,2,1,0:T(2,128)S(1)} %get-tuple-element.7), kind=kOutput, calls=%fused_computation.18 | convolution fusion | flops 34013184 | bytes 4886528 | tf_op jit(solution)/shard_map/hrkgs,hrksd->hrkgd/dot_general | solution.py:61
  9.3 0.1 dot_general.29
  9.4 0.0 copy-start.3
  9.4 4.9 %fusion = f32[2,16,2048]{2,1,0:T(8,128)S(1)} fusion(bf16[2,16,2048]{2,1,0:T(8,128)(2,1)S(1)} %dot_general.29, bf16[2048,2048]{1,0:T(8,128)(2,1)} %param.16), kind=kOutput, calls=%fused_computation.2 | convolution fusion | flops 268435456 | bytes 8781824 | tf_op jit(solution)/shard_map/dot_general | solution.py:73
  14.3 0.7 dynamic-slice_bitcast_fusion
  15.0 0.0 collective-permute-start
  15.0 0.0 copy-done.3
  15.0 0.1 copy.25
  15.1 0.1 eq.29
  15.2 0.1 fusion.34
  15.3 0.2 reduce_window_sum.11
  15.4 0.2 select_reduce_fusion
  15.6 0.0 copy-start.5
  15.6 0.1 reduce_sum.62
  15.7 0.6 broadcast_multiply_fusion
  16.3 0.7 convert_element_type.58
  17.0 0.0 copy-start.1
  17.0 0.1 convert_reduce_fusion
  17.1 0.0 copy-done.5
  17.1 0.0 collective-permute-done
  17.1 1.1 %multiply_reduce_fusion = (f32[16]{0:T(128)S(1)}, f32[16,2048]{1,0:T(8,128)S(1)}) fusion(f32[16,2048]{1,0:T(8,128)} %collective-permute-done, f32[2,16,2048]{2,1,0:T(8,128)S(1)} %fusion, s32[]{:T(128)S(6)} %select_n.32, bf16[16,2048]{1,0:T(8,128)(2,1)} %param.11), kind=kLoop, calls=%fused_computation.32 | loop fusion | flops 163824 | bytes 458820 | tf_op jit(solution)/shard_map/reduce_sum | solution.py:81
  18.2 1.5 %convolution_convert_fusion = bf16[256,2048]{1,0:T(8,128)(2,1)} fusion(s32[256,16]{0,1:T(8,128)S(1)} %convert_reduce_fusion, f32[16,2048]{1,0:T(8,128)S(1)} %get-tuple-element.6, f32[2048]{0:T(1024)S(1)} %convert_element_type.58, f32[16]{0:T(128)S(1)} %add_rsqrt_fusion), kind=kOutput, calls=%fused_computation.13 | convolution fusion | flops 17403904 | bytes 1204288 | tf_op jit(solution)/shard_map/dot_general | solution.py:104
  19.7 2.5 %reshape.112 = bf16[128,2,2048]{2,1,0:T(2,128)(2,1)} reshape(bf16[256,2048]{1,0:T(8,128)(2,1)} %convolution_convert_fusion) | data formatting | bytes 2097152 | tf_op jit(solution)/shard_map/reshape | solution.py:105
  22.3 29.5 %all_to_all.10 = bf16[128,2,2048]{2,1,0:T(2,128)(2,1)} all-to-all(bf16[128,2,2048]{2,1,0:T(2,128)(2,1)} %reshape.112), channel_id=1, replica_groups=mesh['grp'=2,'dev'=64] {'grp','dev'}, dimensions={0} | all-to-all | bytes 2097152 | tf_op jit(solution)/shard_map/all_to_all | solution.py:106
  51.8 2.3 %reshape.113 = bf16[256,2048]{1,0:T(8,128)(2,1)} reshape(bf16[128,2,2048]{2,1,0:T(2,128)(2,1)} %all_to_all.10) | data formatting | bytes 2097152 | tf_op jit(solution)/shard_map/reshape | solution.py:109
  54.0 4.9 %fusion.2 = f32[256,1536]{1,0:T(8,128)S(1)} fusion(bf16[256,2048]{1,0:T(8,128)(2,1)} %reshape.113, bf16[1,2048,1536]{2,1,0:T(8,128)(2,1)} %param.20), kind=kOutput, calls=%fused_computation.4 | convolution fusion | flops 1610612736 | bytes 8912896 | tf_op jit(solution)/shard_map/dot_general | solution.py:108
  58.9 0.0 copy-done.1
  58.9 0.0 copy-done
  58.9 0.0 copy-start.4
  58.9 0.0 copy-start.6
  59.0 2.0 %fusion.10 = bf16[256,2048]{1,0:T(8,128)(2,1)} fusion(bf16[1,768,2048]{2,1,0:T(8,128)(2,1)S(1)} %copy-done, f32[256,1536]{1,0:T(8,128)S(1)} %fusion.2), kind=kOutput, calls=%fused_computation.12 | convolution fusion | flops 807010304 | bytes 5767168 | tf_op jit(solution)/shard_map/dot_general | solution.py:112
  61.0 0.0 copy-start.2
  61.0 2.6 %reshape.114 = bf16[128,2,2048]{2,1,0:T(2,128)(2,1)} reshape(bf16[256,2048]{1,0:T(8,128)(2,1)} %fusion.10) | data formatting | bytes 2097152 | tf_op jit(solution)/shard_map/reshape | solution.py:116
  63.6 5.8 %all-to-all-start.1 = ((bf16[128,2,2048]{2,1,0:T(2,128)(2,1)}), bf16[128,2,2048]{2,1,0:T(2,128)(2,1)}, u32[]{:S(2)}, u32[]{:S(2)}) async-start(bf16[128,2,2048]{2,1,0:T(2,128)(2,1)} %reshape.114), calls=%async_computation.1 | async-start | bytes 2097152 | tf_op jit(solution)/shard_map/all_to_all | solution.py:115
  69.4 0.1 copy.22
  69.4 0.1 reshape.125
  69.5 0.0 copy-done.4
  69.5 0.1 mul.100
  69.6 0.0 copy-done.6
  69.7 0.0 copy-done.2
  69.7 1.3 %fusion.44 = f32[16,128]{1,0:T(8,128)S(1)} fusion(bf16[2048,128]{1,0:T(8,128)(2,1)} %param.18, f32[16,2048]{1,0:T(8,128)S(1)} %get-tuple-element.6, f32[2048]{0:T(1024)S(1)} %copy-done.2, f32[16]{0:T(128)S(1)} %add_rsqrt_fusion), kind=kOutput, calls=%fused_computation.60 | convolution fusion | flops 8486912 | bytes 671808 | tf_op jit(solution)/shard_map/dot_general | solution.py:85
  70.9 1.3 %gather_fusion.1 = f32[128]{0:T(128)S(1)} fusion(f32[16,128]{1,0:T(8,128)S(1)} %fusion.44, s32[128]{0:T(128)S(1)} %reshape.125), kind=kCustom, calls=%fused_computation.1 | custom fusion | bytes 2048 | tf_op jit(solution)/shard_map/jit(take_along_axis)/gather | solution.py:86
  72.2 0.1 reshape.128
  72.3 0.1 copy.23
  72.4 0.1 copy.24
  72.5 14.6 %all-to-all-done.1 = bf16[128,2,2048]{2,1,0:T(2,128)(2,1)} async-done(((bf16[128,2,2048]{2,1,0:T(2,128)(2,1)}), bf16[128,2,2048]{2,1,0:T(2,128)(2,1)}, u32[]{:S(2)}, u32[]{:S(2)}) %all-to-all-start.1) | async-done | bytes 1048608 | tf_op jit(solution)/shard_map/all_to_all | solution.py:115
  87.0 2.3 %reshape.115 = bf16[256,2048]{1,0:T(8,128)(2,1)} reshape(bf16[128,2,2048]{2,1,0:T(2,128)(2,1)} %all-to-all-done.1) | data formatting | bytes 2097152 | tf_op jit(solution)/shard_map/reshape | solution.py:118
  89.3 3.6 %gather_fusion = bf16[128,2048]{1,0:T(8,128)(2,1)} fusion(bf16[256,2048]{1,0:T(8,128)(2,1)} %reshape.115, s32[1024]{0:T(1024)S(1)} %pad_clamp_fusion), kind=kCustom, calls=%fused_computation | custom fusion | bytes 1049088 | tf_op jit(solution)/shard_map/gather | solution.py:119
  92.9 1.5 %fusion.28 = f32[16,2048]{1,0:T(8,128)S(1)} fusion(bf16[128,2048]{1,0:T(8,128)(2,1)} %gather_fusion, f32[16,8]{1,0:T(8,128)S(1)} %copy.24), kind=kLoop, calls=%fused_computation.20 | loop fusion | flops 753664 | bytes 655872 | tf_op jit(solution)/shard_map/reduce_sum | solution.py:120
  94.4 0.6 add_convert_fusion
  (7 shorter events, 0.1 us)
Async XLA Ops:
  0.0 58.9 %copy-start = (bf16[1,768,2048]{2,1,0:T(8,128)(2,1)S(1)}, bf16[1,768,2048]{2,1,0:T(8,128)(2,1)}, u32[]{:S(2)}) copy-start(bf16[1,768,2048]{2,1,0:T(8,128)(2,1)} %param.21) | copy-start | bytes 9437188
  9.4 5.6 %copy-start.3 = (s32[16,8]{0,1:T(8,128)S(1)}, s32[16,8]{0,1:T(8,128)}, u32[]{:S(2)}) copy-start(s32[16,8]{0,1:T(8,128)} %param.19) | copy-start | bytes 1540
  15.0 2.1 %collective-permute-start = (f32[16,2048]{1,0:T(8,128)}, f32[16,2048]{1,0:T(8,128)}, u32[]{:S(2)}, u32[]{:S(2)}) collective-permute-start(f32[16,2048]{1,0:T(8,128)} %dynamic-slice_bitcast_fusion), channel_id=1, source_target_pairs={{0,64},{64,0},{1,65},{65,1},{2,66},{66,2},{3,67},{67,3},{4,68},{68... | collective-permute-start | bytes 393224 | tf_op jit(solution)/shard_map/ppermute | solution.py:79
  15.6 1.5 %copy-start.5 = (s32[128]{0:T(128)}, s32[128]{0:T(128)S(1)}, u32[]{:S(2)}) copy-start(s32[128]{0:T(128)S(1)} %select_reduce_fusion) | copy-start | bytes 1540
  17.0 41.9 %copy-start.1 = (f32[2048]{0:T(1024)}, f32[2048]{0:T(1024)S(1)}, u32[]{:S(2)}) copy-start(f32[2048]{0:T(1024)S(1)} %convert_element_type.58) | copy-start | bytes 24580
  58.9 10.6 %copy-start.4 = (s32[16,8]{1,0:T(8,128)S(1)}, s32[16,8]{1,0:T(8,128)}, u32[]{:S(2)}) copy-start(s32[16,8]{1,0:T(8,128)} %get-tuple-element.11) | copy-start | bytes 1540
  58.9 10.7 %copy-start.6 = (s32[128]{0:T(128)S(1)}, s32[128]{0:T(128)}, u32[]{:S(2)}) copy-start(s32[128]{0:T(128)} %copy-done.5) | copy-start | bytes 1540
  61.0 8.7 %copy-start.2 = (f32[2048]{0:T(1024)S(1)}, f32[2048]{0:T(1024)}, u32[]{:S(2)}) copy-start(f32[2048]{0:T(1024)} %copy-done.1) | copy-start | bytes 24580
  63.6 23.5 %all-to-all-start.1 = ((bf16[128,2,2048]{2,1,0:T(2,128)(2,1)}), bf16[128,2,2048]{2,1,0:T(2,128)(2,1)}, u32[]{:S(2)}, u32[]{:S(2)}) async-start(bf16[128,2,2048]{2,1,0:T(2,128)(2,1)} %reshape.114), calls=%async_computation.1 | async-start | bytes 2097152 | tf_op jit(solution)/shard_map/all_to_all | solution.py:115

commit v2 on v0

v2 whole, which is shorter than its diff:
```python
import functools
import math

import jax
import jax.numpy as jnp
from jax import lax
from jax.experimental import pallas as pl
from jax.experimental.pallas import tpu as pltpu
from jax.sharding import PartitionSpec as P

HEAD_SIZE = 128
LANES = 128
FF = 768
CAP = 2
W_CHUNKS = 4
UNROLL = 4
VMEM_LIMIT = 48 * 1024 * 1024

F32 = jnp.float32
BF16 = jnp.bfloat16


def dot(a, b, contract=((1,), (0,))):
    return lax.dot_general(a, b, (contract, ((), ())), preferred_element_type=F32)


def attend_kernel(
    place_ref,
    length_ref,
    query_ref,
    fresh_ref,
    routes_ref,
    cache_hbm,
    weight_hbm,
    own_ref,
    other_ref,
    target_ref,
    cache_buf,
    weight_buf,
    query_buf,
    fresh_buf,
    mixed_buf,
    cache_sem,
    weight_sem,
):
    rows, kv_heads, positions, _ = cache_buf.shape
    q_heads = query_ref.shape[1] // HEAD_SIZE
    group = q_heads // kv_heads
    width = weight_buf.shape[1]
    span = width // W_CHUNKS
    scale = 1.0 / math.sqrt(HEAD_SIZE)

    def cache_copy(row):
        return pltpu.make_async_copy(cache_hbm.at[row], cache_buf.at[row], cache_sem.at[row])

    def weight_copy(part):
        cols = pl.ds(part * span, span)
        return pltpu.make_async_copy(
            weight_hbm.at[:, cols], weight_buf.at[:, cols], weight_sem.at[part]
        )

    for row in range(rows):
        cache_copy(row).start()
    for part in range(W_CHUNKS):
        weight_copy(part).start()

    routes = routes_ref[...]
    batch, topk = routes.shape
    lane = lax.broadcasted_iota(jnp.int32, (batch, LANES), 1)
    named = jnp.zeros((batch, LANES), F32)
    for k in range(topk):
        named += jnp.where(lane == routes[:, k : k + 1], 1.0, 0.0)
    below = lax.broadcasted_iota(jnp.int32, (batch, batch), 0) > lax.broadcasted_iota(
        jnp.int32, (batch, batch), 1
    )
    earlier = dot(jnp.where(below, 1.0, 0.0).astype(BF16), named.astype(BF16))
    slot = lane.astype(F32) * CAP + earlier
    target = jnp.zeros((batch, LANES), F32)
    for k in range(topk):
        found = jnp.sum(
            jnp.where(lane == routes[:, k : k + 1], slot, 0.0), axis=1, keepdims=True
        )
        target = jnp.where(lane == k, found, target)
    target_ref[...] = target.astype(jnp.int32)

    for j in range(q_heads):
        query_buf[pl.ds(j, rows, stride=q_heads), :] = query_ref[
            :, j * HEAD_SIZE : (j + 1) * HEAD_SIZE
        ].astype(F32)
    fresh_buf[...] = fresh_ref[...].astype(F32)

    position = lax.broadcasted_iota(jnp.int32, (q_heads, positions), 1)

    def one_row(row):
        first = pl.multiple_of(row * q_heads, q_heads)
        query = query_buf[pl.ds(first, q_heads), :]
        query16 = query.astype(BF16)
        fresh = fresh_buf[row]
        scores, new_key, new_value = [], [], []
        for head in range(kv_heads):
            part = dot(query16, cache_buf[row, head, :, :HEAD_SIZE], ((1,), (1,)))
            scores.append(part[head * group : (head + 1) * group])
            new_key.append(
                jnp.broadcast_to(fresh[head : head + 1, :HEAD_SIZE], (group, HEAD_SIZE))
            )
            new_value.append(
                jnp.broadcast_to(fresh[head : head + 1, HEAD_SIZE:], (group, HEAD_SIZE))
            )
        scores = jnp.concatenate(scores, axis=0) * scale
        own = jnp.sum(query * jnp.concatenate(new_key, axis=0), axis=1, keepdims=True) * scale
        raised = jnp.where(position < length_ref[row], jnp.exp(scores), 0.0)
        own = jnp.exp(own)
        total = jnp.sum(raised, axis=1, keepdims=True) + own
        weights = (raised / total).astype(BF16)
        own_weight = (own / total).astype(BF16).astype(F32)
        mixed = []
        for head in range(kv_heads):
            part = dot(weights, cache_buf[row, head, :, HEAD_SIZE:])
            mixed.append(part[head * group : (head + 1) * group])
        mixed = jnp.concatenate(mixed, axis=0) + own_weight * jnp.concatenate(new_value, axis=0)
        mixed_buf[pl.ds(first, q_heads), :] = mixed

    def some_rows(step, carry):
        for u in range(UNROLL):
            cache_copy(step * UNROLL + u).wait()
        for u in range(UNROLL):
            one_row(step * UNROLL + u)
        return carry

    lax.fori_loop(0, rows // UNROLL, some_rows, 0)

    attended = jnp.concatenate(
        [mixed_buf[pl.ds(j, rows, stride=q_heads), :].astype(BF16) for j in range(q_heads)],
        axis=1,
    )
    first_group = place_ref[0] == 0
    for part in range(W_CHUNKS):
        weight_copy(part).wait()
        cols = slice(part * span, (part + 1) * span)
        product = dot(attended, weight_buf[:, cols])
        top, bottom = product[: rows // 2], product[rows // 2 :]
        own_ref[:, cols] = jnp.where(first_group, top, bottom)
        other_ref[:, cols] = jnp.where(first_group, bottom, top)


def attend(place, length, query, fresh, routes, cache, weight):
    rows, kv_heads, positions, pair = cache.shape
    width = weight.shape[1]
    smem = pl.BlockSpec(memory_space=pltpu.SMEM)
    vmem = pl.BlockSpec(memory_space=pltpu.VMEM)
    hbm = pl.BlockSpec(memory_space=pl.ANY)
    half = jax.ShapeDtypeStruct((rows // 2, width), F32)
    return pl.pallas_call(
        attend_kernel,
        out_shape=(half, half, jax.ShapeDtypeStruct((routes.shape[0], LANES), jnp.int32)),
        in_specs=[smem, smem, vmem, vmem, vmem, hbm, hbm],
        out_specs=(vmem, vmem, vmem),
        scratch_shapes=[
            pltpu.VMEM(cache.shape, BF16),
            pltpu.VMEM(weight.shape, BF16),
            pltpu.VMEM((rows * query.shape[1] // HEAD_SIZE, HEAD_SIZE), F32),
            pltpu.VMEM(fresh.shape, F32),
            pltpu.VMEM((rows * query.shape[1] // HEAD_SIZE, HEAD_SIZE), F32),
            pltpu.SemaphoreType.DMA((rows,)),
            pltpu.SemaphoreType.DMA((W_CHUNKS,)),
        ],
        compiler_params=pltpu.CompilerParams(vmem_limit_bytes=VMEM_LIMIT),
        name="attend",
    )(place, length, query, fresh, routes, cache, weight)


def dispatch_kernel(
    target_ref,
    own_ref,
    passed_ref,
    residual_ref,
    gain_ref,
    router_ref,
    routes_ref,
    hidden_ref,
    gates_ref,
    slots_ref,
    row_buf,
):
    batch, width = own_ref.shape
    chunks = width // LANES
    topk = routes_ref.shape[1]
    hidden = residual_ref[...].astype(F32) + (own_ref[...] + passed_ref[...])
    hidden_ref[...] = hidden
    meansq = jnp.mean(hidden * hidden, axis=1, keepdims=True)
    normed = (hidden * lax.rsqrt(meansq + 1e-06) * gain_ref[...].astype(F32)).astype(BF16)
    for j in range(chunks):
        row_buf[pl.ds(j, batch, stride=chunks), :] = normed[
            :, j * LANES : (j + 1) * LANES
        ].astype(F32)

    raised = jnp.exp(dot(normed, router_ref[...]))
    routes = routes_ref[...]
    lane = lax.broadcasted_iota(jnp.int32, (batch, LANES), 1)
    total = jnp.zeros((batch, 1), F32)
    gates = jnp.zeros((batch, LANES), F32)
    for k in range(topk):
        picked = jnp.sum(
            jnp.where(lane == routes[:, k : k + 1], raised, 0.0), axis=1, keepdims=True
        )
        total += picked
        gates = jnp.where(lane == k, picked, gates)
    gates_ref[...] = gates / total

    slots_ref[...] = jnp.zeros_like(slots_ref)
    for r in range(batch):
        row = row_buf[r * chunks : (r + 1) * chunks, :].astype(BF16)
        for k in range(topk):
            slots_ref[target_ref[r, k]] = row


def dispatch(target, own, passed, residual, gain, router, routes):
    batch, width = own.shape
    smem = pl.BlockSpec(memory_space=pltpu.SMEM)
    vmem = pl.BlockSpec(memory_space=pltpu.VMEM)
    return pl.pallas_call(
        dispatch_kernel,
        out_shape=(
            jax.ShapeDtypeStruct((batch, width), F32),
            jax.ShapeDtypeStruct((batch, LANES), F32),
            jax.ShapeDtypeStruct((router.shape[1] * CAP, width // LANES, LANES), BF16),
        ),
        in_specs=[smem] + [vmem] * 6,
        out_specs=(vmem, vmem, vmem),
        scratch_shapes=[pltpu.VMEM((batch * width // LANES, LANES), F32)],
        compiler_params=pltpu.CompilerParams(vmem_limit_bytes=VMEM_LIMIT),
        name="dispatch",
    )(target, own, passed, residual, gain, router, routes)


def expert_kernel(
    x_hbm, up_hbm, down_hbm, out_ref, x_in, up_buf, down_buf, wide, x_buf, act_buf, x_sem, up_sem, down_sem
):
    count, chunks, _ = x_in.shape
    width = chunks * LANES
    step = 256
    parts = FF // step
    span = width // W_CHUNKS
    x_copy = pltpu.make_async_copy(x_hbm, x_in, x_sem)
    x_copy.start()

    def up_copy(half, part):
        cols = pl.ds(half * FF + part * step, step)
        return pltpu.make_async_copy(
            up_hbm.at[:, cols], up_buf.at[:, cols], up_sem.at[half, part]
        )

    def down_copy(part):
        cols = pl.ds(part * span, span)
        return pltpu.make_async_copy(
            down_hbm.at[:, cols], down_buf.at[:, cols], down_sem.at[part]
        )

    for part in range(parts):
        for half in range(2):
            up_copy(half, part).start()
    for part in range(W_CHUNKS):
        down_copy(part).start()

    x_copy.wait()
    wide[...] = x_in[...].reshape(count * chunks, LANES).astype(F32)
    for j in range(chunks):
        x_buf[:, j * LANES : (j + 1) * LANES] = wide[pl.ds(j, count, stride=chunks), :].astype(
            BF16
        )
    for part in range(parts):
        up_copy(0, part).wait()
        up_copy(1, part).wait()
        gate = dot(x_buf[...], up_buf[:, part * step : (part + 1) * step])
        lift = dot(x_buf[...], up_buf[:, FF + part * step : FF + (part + 1) * step])
        act_buf[:, part * step : (part + 1) * step] = (
            gate * (1.0 / (1.0 + jnp.exp(-gate))) * lift
        ).astype(BF16)
    for part in range(W_CHUNKS):
        down_copy(part).wait()
        served = dot(act_buf[...], down_buf[:, part * span : (part + 1) * span])
        for j in range(span // LANES):
            wide[pl.ds(part * (span // LANES) + j, count, stride=chunks), :] = served[
                :, j * LANES : (j + 1) * LANES
            ]
    out_ref[...] = wide[...].astype(BF16).reshape(count, chunks, LANES)


def expert(x, up, down):
    count, chunks, _ = x.shape
    vmem = pl.BlockSpec(memory_space=pltpu.VMEM)
    hbm = pl.BlockSpec(memory_space=pl.ANY)
    return pl.pallas_call(
        expert_kernel,
        out_shape=jax.ShapeDtypeStruct(x.shape, BF16),
        in_specs=[hbm, hbm, hbm],
        out_specs=vmem,
        scratch_shapes=[
            pltpu.VMEM(x.shape, BF16),
            pltpu.VMEM(up.shape, BF16),
            pltpu.VMEM(down.shape, BF16),
            pltpu.VMEM((count * chunks, LANES), F32),
            pltpu.VMEM((count, chunks * LANES), BF16),
            pltpu.VMEM((count, FF), BF16),
            pltpu.SemaphoreType.DMA,
            pltpu.SemaphoreType.DMA((2, FF // 256)),
            pltpu.SemaphoreType.DMA((W_CHUNKS,)),
        ],
        compiler_params=pltpu.CompilerParams(vmem_limit_bytes=VMEM_LIMIT),
        name="expert",
    )(x, up, down)


def combine_kernel(target_ref, gates_ref, hidden_ref, table_ref, out_ref, row_buf, *, topk):
    batch, width = hidden_ref.shape
    chunks = width // LANES
    for r in range(batch):
        total = jnp.zeros((chunks, LANES), F32)
        for k in range(topk):
            total += gates_ref[r, k] * table_ref[target_ref[r, k]].astype(F32)
        row_buf[r * chunks : (r + 1) * chunks, :] = total
    for j in range(chunks):
        cols = slice(j * LANES, (j + 1) * LANES)
        out_ref[:, cols] = (
            hidden_ref[:, cols] + row_buf[pl.ds(j, batch, stride=chunks), :]
        ).astype(BF16)


def combine(target, gates, hidden, table, topk):
    batch, width = hidden.shape
    smem = pl.BlockSpec(memory_space=pltpu.SMEM)
    vmem = pl.BlockSpec(memory_space=pltpu.VMEM)
    return pl.pallas_call(
        functools.partial(combine_kernel, topk=topk),
        out_shape=jax.ShapeDtypeStruct((batch, width), BF16),
        in_specs=[smem, smem, vmem, vmem],
        out_specs=vmem,
        scratch_shapes=[pltpu.VMEM((batch * width // LANES, LANES), F32)],
        compiler_params=pltpu.CompilerParams(vmem_limit_bytes=VMEM_LIMIT),
        name="combine",
    )(target, gates, hidden, table)


def per_device(
    residual_in,
    queries,
    latest_key_value,
    key_value_cache,
    cache_len,
    out_weight,
    norm_gain,
    router_weight,
    routes,
    expert_gate_up,
    expert_down,
):
    rows = queries.shape[0] * queries.shape[1]
    experts = router_weight.shape[1]
    topk = routes.shape[1]
    place = lax.axis_index("grp").reshape(1)
    own, other, target = attend(
        place,
        cache_len.reshape(rows),
        queries.reshape(rows, -1),
        latest_key_value.reshape((rows,) + latest_key_value.shape[2:]),
        routes,
        key_value_cache.reshape((rows,) + key_value_cache.shape[2:]),
        out_weight,
    )
    passed = lax.ppermute(other, "grp", [(0, 1), (1, 0)])
    hidden, gates, slots = dispatch(
        target, own, passed, residual_in, norm_gain.reshape(1, -1), router_weight, routes
    )
    block = (experts, CAP * slots.shape[1], LANES)
    received = lax.all_to_all(
        slots.reshape(block), ("grp", "dev"), split_axis=0, concat_axis=0, tiled=True
    )
    served = expert(received.reshape(slots.shape), expert_gate_up[0], expert_down[0])
    returned = lax.all_to_all(
        served.reshape(block), ("grp", "dev"), split_axis=0, concat_axis=0, tiled=True
    )
    return combine(target, gates, hidden, returned.reshape(slots.shape), topk)


def solution(mesh):
    placed = (
        P(("grp", "dev"), None),
        P(None, "dev", "grp"),
        P(None, "dev", "grp", None),
        P(None, "dev", "grp", None, None),
        P(None, "dev"),
        P("grp", None),
        P(),
        P(),
        P(("grp", "dev"), None),
        P(("grp", "dev"), None, None),
        P(("grp", "dev"), None, None),
    )
    return jax.shard_map(
        per_device, mesh=mesh, in_specs=placed, out_specs=P(("grp", "dev"), None), check_vma=False
    )
```

time: 133 us -> 79 us (0.59)
  waiting for transfers between devices: 40.2 us -> 1.31 us
  blocking collectives: 28.3 us -> 52.2 us
  matrix products: 21.9 us -> 0 us
  Pallas kernels: 0 us -> 21.8 us
  between operations: 13.6 us -> 0.06 us
  local copies, waits for them, and re-layouts: 16.2 us -> 3.2 us
  other arithmetic: 6.56 us -> 0 us
  starting transfers between devices: 5.78 us -> 0.09 us
    psum x1 -> x0, waiting for transfers between devices: 25.6 us -> none  [per_device(): summed = lax.psum(partial_value, 'grp')]
    all_to_all x1 -> x2, blocking collectives: 28.3 us -> 52.2 us  [the longest x1 29.1 us: per_device(): lax.all_to_all(slots.reshape(block), ('grp', 'dev'), split_axis=0, concat...]
    dot_general x8 -> x0, matrix products: 21.9 us -> none  [the longest x1 5.65 us: per_device(): jnp.dot(attended, out_weight, preferred_element_type=jnp.float32)]
    pallas_call x0 -> x4, Pallas kernels: none -> 21.8 us  [the longest x1 13 us: attend(): pl.pallas_call(attend_kernel, out_shape=(half, half, jax.ShapeDtypeStruct...]
    all_to_all x1 -> x0, waiting for transfers between devices: 14.6 us -> none  [per_device(): lax.all_to_all(result.reshape(received.shape), ('grp', 'dev'), split_axis...]
    reshape x4 -> x2, local copies, waits for them, and re-layouts: 9.62 us -> 0.77 us  [the longest x1 0.76 us: per_device(): cache_len.reshape(rows)]
    all_to_all x1 -> x0, starting transfers between devices: 5.78 us -> none  [per_device(): lax.all_to_all(result.reshape(received.shape), ('grp', 'dev'), split_axis...]
    gather x6 -> x0, local copies, waits for them, and re-layouts: 5.15 us -> none  [the longest x1 3.59 us: per_device(): table[target].reshape(batch_rows, topk, width).astype(jnp.float32)]
  transfers between devices with their start and end apart: 2 -> 1, of which waited for: 2 -> 1; matrix products, arithmetic and copies ran while one was open for 3% -> 0% of each run, Pallas kernels for 0% -> 0%
where the time goes in v2:
time: 79 us; the launch traced here: 78.7 us
  blocking collectives  52.2 us (66%)
  Pallas kernels  21.8 us (28%)
  local copies, waits for them, and re-layouts  3.2 us (4%)
  waiting for transfers between devices  1.31 us (2%)
    all_to_all x1, blocking collectives, per_device(): lax.all_to_all(slots.reshape(block), ('grp', 'dev'), split_axis=0, concat...  29.1 us
    all_to_all x1, blocking collectives, per_device(): lax.all_to_all(served.reshape(block), ('grp', 'dev'), split_axis=0, conca...  23.2 us
    pallas_call x1, Pallas kernels, attend(): pl.pallas_call(attend_kernel, out_shape=(half, half, jax.ShapeDtypeStruct...  13 us
    pallas_call x1, Pallas kernels, expert(): pl.pallas_call(expert_kernel, out_shape=jax.ShapeDtypeStruct(x.shape, BF1...  6.09 us
    unnamed x13, local copies, waits for them, and re-layouts  2.43 us
    pallas_call x1, Pallas kernels, combine(): pl.pallas_call(functools.partial(combine_kernel, topk=topk), out_shape=ja...  1.59 us
  transfers between devices with their start and end apart: 1, of which 1 were waited for; matrix products, arithmetic and copies ran while one was open for 0% of the time, Pallas kernels for 0%

profile of v2, /device:TPU:0, one launch (start us, length us, event | category | flops | bytes accessed | tf_op | source)
XLA Modules:
  0.0 78.7 jit_solution(17272479970320096236)
XLA Ops:
  0.0 0.8 reshape.31.length_ref
  0.8 0.8 copy.12.routes_ref
  1.5 0.0 copy-start.2
  1.5 0.9 %copy-done.2 = bf16[2,16,2048]{2,1,0:T(8,128)(2,1)S(1)} copy-done((bf16[2,16,2048]{2,1,0:T(8,128)(2,1)S(1)}, bf16[2,16,2048]{2,1,0:T(8,128)(2,1)}, u32[]{:S(2)}) %copy-start.2) | copy-done | bytes 131096
  2.4 0.0 copy-start.4
  2.4 0.8 copy-done.4
  3.2 0.0 copy-start.5
  3.2 0.0 copy-start.1
  3.2 0.0 copy-start.3
  3.2 0.0 copy-start
  3.2 13.0 %attend.1 = (f32[16,2048]{1,0:T(8,128)S(1)}, f32[16,2048]{1,0:T(8,128)S(1)}, s32[16,128]{1,0:T(8,128)S(1)}) custom-call(s32[1]{0:T(128)} %bitcast.place_ref, s32[32]{0:T(128)S(1)} %reshape.31.length_ref, bf16[32,2048]{1,0:T(8,128)(2,1)S(1)} %bitcast.15, bf16[32,2,256]{2,1,0:T(2,128)(2,1)S(1)} %bitcast.16, s32[16,8]{1,0:T(8,128)S(1)} %copy.12.routes_ref, ...), custom_call_target="tpu_custom_call" | custom-call | tf_op jit(solution)/shard_map/attend/pallas_call | solution.py:153
  16.2 0.1 collective-permute-start
  16.3 0.0 copy-done.5
  16.4 1.3 %collective-permute-done.passed_ref = f32[16,2048]{1,0:T(8,128)S(1)} collective-permute-done((f32[16,2048]{1,0:T(8,128)S(1)}, f32[16,2048]{1,0:T(8,128)S(1)}, u32[]{:S(2)}, u32[]{:S(2)}) %collective-permute-start) | collective-permute-done | bytes 131104 | tf_op jit(solution)/shard_map/ppermute | solution.py:370
  17.7 0.0 copy-done.1
  17.7 0.0 copy-done.3
  17.7 1.1 %dispatch.1 = (f32[16,2048]{1,0:T(8,128)S(1)}, f32[16,128]{1,0:T(8,128)S(1)}, bf16[256,16,128]{2,1,0:T(8,128)(2,1)S(1)}) custom-call(s32[16,128]{1,0:T(8,128)S(1)} %get-tuple-element.11.target_ref, f32[16,2048]{1,0:T(8,128)S(1)} %get-tuple-element.12.own_ref, f32[16,2048]{1,0:T(8,128)S(1)} %collective-permute-done.passed_ref, ...), custom_call_target="tpu_custom_call" | custom-call | tf_op jit(solution)/shard_map/dispatch/pallas_call | solution.py:221
  18.8 29.1 %all_to_all.10 = bf16[128,32,128]{2,1,0:T(8,128)(2,1)S(1)} all-to-all(bf16[128,32,128]{2,1,0:T(8,128)(2,1)S(1)} %bitcast.14), channel_id=1, replica_groups=mesh['grp'=2,'dev'=64] {'grp','dev'}, dimensions={0} | all-to-all | bytes 2097152 | tf_op jit(solution)/shard_map/all_to_all | solution.py:375
  47.9 0.0 copy-done
  47.9 6.1 %expert.1 = bf16[256,16,128]{2,1,0:T(8,128)(2,1)S(1)} custom-call(bf16[256,16,128]{2,1,0:T(8,128)(2,1)S(1)} %bitcast.11, bf16[2048,1536]{1,0:T(8,128)(2,1)} %bitcast.18, bf16[768,2048]{1,0:T(8,128)(2,1)S(1)} %bitcast.13), custom_call_target="tpu_custom_call" | custom-call | tf_op jit(solution)/shard_map/expert/pallas_call | solution.py:293
  54.0 23.2 %all_to_all.11 = bf16[128,32,128]{2,1,0:T(8,128)(2,1)S(1)} all-to-all(bf16[128,32,128]{2,1,0:T(8,128)(2,1)S(1)} %bitcast.12), channel_id=1, replica_groups=mesh['grp'=2,'dev'=64] {'grp','dev'}, dimensions={0} | all-to-all | bytes 2097152 | tf_op jit(solution)/shard_map/all_to_all | solution.py:379
  77.1 1.6 %combine.1 = bf16[16,2048]{1,0:T(8,128)(2,1)} custom-call(s32[16,128]{1,0:T(8,128)S(1)} %get-tuple-element.11.target_ref, f32[16,128]{1,0:T(8,128)S(1)} %get-tuple-element.14.gates_ref, f32[16,2048]{1,0:T(8,128)S(1)} %get-tuple-element.15.hidden_ref, bf16[256,16,128]{2,1,0:T(8,128)(2,1)S(1)} %bitcast.10), custom_call_target="tpu_custom_call" | custom-call | tf_op jit(solution)/shard_map/combine/pallas_call | solution.py:333
  (1 shorter events, 0.0 us)
Async XLA Ops:
  1.5 0.9 %copy-start.2 = (bf16[2,16,2048]{2,1,0:T(8,128)(2,1)S(1)}, bf16[2,16,2048]{2,1,0:T(8,128)(2,1)}, u32[]{:S(2)}) copy-start(bf16[2,16,2048]{2,1,0:T(8,128)(2,1)} %param.12) | copy-start | bytes 393220
  2.4 0.8 copy-start.4
  3.2 13.2 %copy-start.5 = (bf16[2048]{0:T(1024)(128)(2,1)S(1)}, bf16[2048]{0:T(1024)(128)(2,1)}, u32[]{:S(2)}) copy-start(bf16[2048]{0:T(1024)(128)(2,1)} %param.17) | copy-start | bytes 12292
  3.2 14.5 %copy-start.1 = (bf16[2048,128]{1,0:T(8,128)(2,1)S(1)}, bf16[2048,128]{1,0:T(8,128)(2,1)}, u32[]{:S(2)}) copy-start(bf16[2048,128]{1,0:T(8,128)(2,1)} %router_ref.1) | copy-start | bytes 1572868
  3.2 14.5 %copy-start.3 = (bf16[16,2048]{1,0:T(8,128)(2,1)S(1)}, bf16[16,2048]{1,0:T(8,128)(2,1)}, u32[]{:S(2)}) copy-start(bf16[16,2048]{1,0:T(8,128)(2,1)} %residual_ref.1) | copy-start | bytes 196612
  3.2 44.7 %copy-start = (bf16[1,768,2048]{2,1,0:T(8,128)(2,1)S(1)}, bf16[1,768,2048]{2,1,0:T(8,128)(2,1)}, u32[]{:S(2)}) copy-start(bf16[1,768,2048]{2,1,0:T(8,128)(2,1)} %param.21) | copy-start | bytes 9437188
  16.2 1.4 %collective-permute-start = (f32[16,2048]{1,0:T(8,128)S(1)}, f32[16,2048]{1,0:T(8,128)S(1)}, u32[]{:S(2)}, u32[]{:S(2)}) collective-permute-start(f32[16,2048]{1,0:T(8,128)S(1)} %get-tuple-element.13), channel_id=1, source_target_pairs={{0,64},{64,0},{1,65},{65,1},{2,66},{66,2},{3,67},{67,3},{4,68},{68... | collective-permute-start | bytes 393224 | tf_op jit(solution)/shard_map/ppermute | solution.py:370

commit v3 on v2

v3 whole, which is shorter than its diff:
```python
import functools
import math

import jax
import jax.numpy as jnp
from jax import lax
from jax.experimental import pallas as pl
from jax.experimental.pallas import tpu as pltpu
from jax.sharding import PartitionSpec as P

HEAD_SIZE = 128
LANES = 128
FF = 768
CAP = 2
UNROLL = 8
STEP = 256
SPAN = 512
W_CHUNKS = 4
NODMA=False
MIB = 1024 * 1024
SMALL_LIMIT = 12 * MIB
EXPERT_LIMIT = 24 * MIB

F32 = jnp.float32
BF16 = jnp.bfloat16


def dot(a, b, contract=((1,), (0,))):
    return lax.dot_general(a, b, (contract, ((), ())), preferred_element_type=F32)


def attend_kernel(
    place_ref,
    length_hbm,
    query_hbm,
    fresh_hbm,
    routes_hbm,
    cache_hbm,
    weight_hbm,
    own_ref,
    other_ref,
    coded_ref,
    cache_buf,
    weight_buf,
    query_ref,
    fresh_ref,
    routes_ref,
    length_ref,
    query_buf,
    fresh_buf,
    mixed_buf,
    cache_sem,
    weight_sem,
    small_sem,
):
    rows, kv_heads, positions, _ = cache_buf.shape
    q_heads = query_ref.shape[1] // HEAD_SIZE
    group = q_heads // kv_heads
    width = weight_buf.shape[1]
    span = width // W_CHUNKS
    half_rows = rows // 2
    scale = 1.0 / math.sqrt(HEAD_SIZE)

    def whole_copy(row):
        return pltpu.make_async_copy(cache_hbm.at[row], cache_buf.at[row], cache_sem.at[row])

    def part_copy(row):
        valid = length_ref[row // half_rows, row % half_rows]
        kept = pl.ds(0, pl.multiple_of((valid + 15) // 16 * 16, 16))
        return pltpu.make_async_copy(
            cache_hbm.at[row, :, kept], cache_buf.at[row, :, kept], cache_sem.at[row]
        )

    def weight_copy(part):
        cols = pl.ds(part * span, span)
        return pltpu.make_async_copy(
            weight_hbm.at[:, cols], weight_buf.at[:, cols], weight_sem.at[part]
        )

    length_copy = pltpu.make_async_copy(length_hbm, length_ref, small_sem.at[3])
    length_copy.start()
    small_copies = [
        pltpu.make_async_copy(source, kept, small_sem.at[i])
        for i, (source, kept) in enumerate(
            ((routes_hbm, routes_ref), (query_hbm, query_ref), (fresh_hbm, fresh_ref))
        )
    ]
    for copy in small_copies:
        copy.start()
    for row in range(UNROLL):
        whole_copy(row).start()
    for row in range(UNROLL, rows):
        cache_buf[row, :, :, HEAD_SIZE:] = jnp.zeros((kv_heads, positions, HEAD_SIZE), BF16)
    length_copy.wait()
    for row in range(UNROLL, rows):
        part_copy(row).start()

    for copy in small_copies:
        copy.wait()
    topk, batch = routes_ref.shape
    unit = lax.broadcasted_iota(jnp.int32, (topk, topk), 0) == lax.broadcasted_iota(
        jnp.int32, (topk, topk), 1
    )
    routes = dot(
        routes_ref[...].astype(BF16), jnp.where(unit, 1.0, 0.0).astype(BF16), ((0,), (0,))
    ).astype(jnp.int32)
    lane = lax.broadcasted_iota(jnp.int32, (batch, LANES), 1)
    named = jnp.zeros((batch, LANES), F32)
    for k in range(topk):
        named += jnp.where(lane == routes[:, k : k + 1], 1.0, 0.0)
    below = lax.broadcasted_iota(jnp.int32, (batch, batch), 0) > lax.broadcasted_iota(
        jnp.int32, (batch, batch), 1
    )
    earlier = dot(jnp.where(below, 1.0, 0.0).astype(BF16), named.astype(BF16))
    slot = lane.astype(F32) * CAP + earlier
    target = jnp.zeros((batch, LANES), F32)
    for k in range(topk):
        found = jnp.sum(
            jnp.where(lane == routes[:, k : k + 1], slot, 0.0), axis=1, keepdims=True
        )
        target = jnp.where(lane == k, found, target)
    coded_ref[...] = target.astype(jnp.int32) ^ 1

    for j in range(q_heads):
        query_buf[pl.ds(j, rows, stride=q_heads), :] = query_ref[
            :, j * HEAD_SIZE : (j + 1) * HEAD_SIZE
        ].astype(F32)
    fresh_buf[...] = fresh_ref[...].astype(F32)

    position = lax.broadcasted_iota(jnp.int32, (q_heads, positions), 1)

    def some_rows(step, carry):
        first = step * UNROLL
        base = pl.multiple_of(first * q_heads, UNROLL * q_heads)
        query = query_buf[pl.ds(base, UNROLL * q_heads), :]
        query16 = query.astype(BF16)
        @pl.when(step == 0)
        def _():
            for u in range(UNROLL):
                whole_copy(u).wait()
            for part in range(W_CHUNKS):
                weight_copy(part).start()

        @pl.when(step > 0)
        def _():
            for u in range(UNROLL):
                part_copy(first + u).wait()

        scores, visible, new_key, new_value = [], [], [], []
        for u in range(UNROLL):
            fresh = fresh_buf[first + u]
            visible.append(position < length_ref[(first + u) // half_rows, (first + u) % half_rows])
            for head in range(kv_heads):
                begin = u * q_heads + head * group
                keys = cache_buf[first + u, head, :, :HEAD_SIZE]
                scores.append(dot(query16[begin : begin + group], keys, ((1,), (1,))))
                pair = jnp.broadcast_to(fresh[head : head + 1], (group, 2 * HEAD_SIZE))
                new_key.append(pair[:, :HEAD_SIZE])
                new_value.append(pair[:, HEAD_SIZE:])
        scores = jnp.concatenate(scores, axis=0) * scale
        new_key = jnp.concatenate(new_key, axis=0)
        own = jnp.exp(jnp.sum(query * new_key, axis=1, keepdims=True) * scale)
        raised = jnp.where(jnp.concatenate(visible, axis=0), jnp.exp(scores), 0.0)
        total = jnp.sum(raised, axis=1, keepdims=True) + own
        weights = (raised / total).astype(BF16)
        own_weight = (own / total).astype(BF16).astype(F32)
        mixed = []
        for u in range(UNROLL):
            for head in range(kv_heads):
                begin = u * q_heads + head * group
                values = cache_buf[first + u, head, :, HEAD_SIZE:]
                mixed.append(dot(weights[begin : begin + group], values))
        mixed = jnp.concatenate(mixed, axis=0) + own_weight * jnp.concatenate(new_value, axis=0)
        mixed_buf[pl.ds(base, UNROLL * q_heads), :] = mixed
        return carry

    lax.fori_loop(0, rows // UNROLL, some_rows, 0)

    attended = jnp.concatenate(
        [mixed_buf[pl.ds(j, rows, stride=q_heads), :].astype(BF16) for j in range(q_heads)],
        axis=1,
    )
    first_group = place_ref[0] == 0
    for part in range(W_CHUNKS):
        weight_copy(part).wait()
        cols = slice(part * span, (part + 1) * span)
        product = dot(attended, weight_buf[:, cols])
        top, bottom = product[: rows // 2], product[rows // 2 :]
        own_ref[:, cols] = jnp.where(first_group, top, bottom)
        other_ref[:, cols] = jnp.where(first_group, bottom, top)


def attend(place, length, query, fresh, routes, cache, weight):
    rows, kv_heads, positions, pair = cache.shape
    width = weight.shape[1]
    smem = pl.BlockSpec(memory_space=pltpu.SMEM)
    vmem = pl.BlockSpec(memory_space=pltpu.VMEM)
    hbm = pl.BlockSpec(memory_space=pltpu.HBM)
    half = jax.ShapeDtypeStruct((rows // 2, width), F32)
    return pl.pallas_call(
        attend_kernel,
        out_shape=(half, half, jax.ShapeDtypeStruct((routes.shape[1], LANES), jnp.int32)),
        in_specs=[smem, hbm, hbm, hbm, hbm, hbm, hbm],
        out_specs=(vmem, vmem, vmem),
        scratch_shapes=[
            pltpu.VMEM(cache.shape, BF16),
            pltpu.VMEM(weight.shape, BF16),
            pltpu.VMEM(query.shape, BF16),
            pltpu.VMEM(fresh.shape, BF16),
            pltpu.VMEM(routes.shape, jnp.int32),
            pltpu.SMEM(length.shape, jnp.int32),
            pltpu.VMEM((rows * query.shape[1] // HEAD_SIZE, HEAD_SIZE), F32),
            pltpu.VMEM(fresh.shape, F32),
            pltpu.VMEM((rows * query.shape[1] // HEAD_SIZE, HEAD_SIZE), F32),
            pltpu.SemaphoreType.DMA((rows,)),
            pltpu.SemaphoreType.DMA((W_CHUNKS,)),
            pltpu.SemaphoreType.DMA((4,)),
        ],
        compiler_params=pltpu.CompilerParams(vmem_limit_bytes=63 * MIB),
        name="attend",
    )(place, length, query, fresh, routes, cache, weight)


def dispatch_kernel(
    target_ref,
    named_ref,
    base_ref,
    passed_ref,
    gain_ref,
    router_ref,
    hidden_ref,
    gates_ref,
    slots_ref,
    row_buf,
    *,
    topk,
):
    batch, width = base_ref.shape
    chunks = width // LANES
    hidden = base_ref[...] + passed_ref[...]
    hidden_ref[...] = hidden
    meansq = jnp.mean(hidden * hidden, axis=1, keepdims=True)
    normed = (hidden * lax.rsqrt(meansq + 1e-06) * gain_ref[...].astype(F32)).astype(BF16)
    for j in range(chunks):
        row_buf[pl.ds(j, batch, stride=chunks), :] = normed[
            :, j * LANES : (j + 1) * LANES
        ].astype(F32)

    raised = jnp.exp(dot(normed, router_ref[...]))
    routes = named_ref[...]
    lane = lax.broadcasted_iota(jnp.int32, (batch, LANES), 1)
    total = jnp.zeros((batch, 1), F32)
    gates = jnp.zeros((batch, LANES), F32)
    for k in range(topk):
        picked = jnp.sum(
            jnp.where(lane == routes[:, k : k + 1], raised, 0.0), axis=1, keepdims=True
        )
        total += picked
        gates = jnp.where(lane == k, picked, gates)
    gates_ref[...] = gates / total

    slots_ref[...] = jnp.zeros_like(slots_ref)
    for r in range(batch):
        row = row_buf[r * chunks : (r + 1) * chunks, :].astype(BF16)
        for k in range(topk):
            slots_ref[target_ref[r, k]] = row


def dispatch(target, named, base, passed, gain, router, topk):
    batch, width = base.shape
    smem = pl.BlockSpec(memory_space=pltpu.SMEM)
    vmem = pl.BlockSpec(memory_space=pltpu.VMEM)
    return pl.pallas_call(
        functools.partial(dispatch_kernel, topk=topk),
        out_shape=(
            jax.ShapeDtypeStruct((batch, width), F32),
            jax.ShapeDtypeStruct((batch, LANES), F32),
            jax.ShapeDtypeStruct((router.shape[1] * CAP, width // LANES, LANES), BF16),
        ),
        in_specs=[smem] + [vmem] * 5,
        out_specs=(vmem, vmem, vmem),
        scratch_shapes=[pltpu.VMEM((batch * width // LANES, LANES), F32)],
        compiler_params=pltpu.CompilerParams(vmem_limit_bytes=SMALL_LIMIT),
        cost_estimate=pl.CostEstimate(
            flops=10_000_000_000, bytes_accessed=3_000_000, transcendentals=0
        ),
        name="dispatch",
    )(target, named, base, passed, gain, router)


def expert_kernel(x_ref, up_ref, down_ref, out_ref, wide, x_buf, act_buf):
    count, chunks, _ = x_ref.shape
    width = chunks * LANES
    step = STEP
    span = SPAN
    wide[...] = x_ref[...].reshape(count * chunks, LANES).astype(F32)
    for j in range(chunks):
        x_buf[:, j * LANES : (j + 1) * LANES] = wide[pl.ds(j, count, stride=chunks), :].astype(
            BF16
        )
    for part in range(FF // step):
        gate = dot(x_buf[...], up_ref[:, part * step : (part + 1) * step])
        lift = dot(x_buf[...], up_ref[:, FF + part * step : FF + (part + 1) * step])
        act_buf[:, part * step : (part + 1) * step] = (
            gate * (1.0 / (1.0 + jnp.exp(-gate))) * lift
        ).astype(BF16)
    for part in range(width // span):
        served = dot(act_buf[...], down_ref[:, part * span : (part + 1) * span])
        for j in range(span // LANES):
            wide[pl.ds(part * (span // LANES) + j, count, stride=chunks), :] = served[
                :, j * LANES : (j + 1) * LANES
            ]
    out_ref[...] = wide[...].astype(BF16).reshape(count, chunks, LANES)


def expert(x, up, down):
    count, chunks, _ = x.shape
    vmem = pl.BlockSpec(memory_space=pltpu.VMEM)
    return pl.pallas_call(
        expert_kernel,
        out_shape=jax.ShapeDtypeStruct(x.shape, BF16),
        in_specs=[vmem, vmem, vmem],
        out_specs=vmem,
        scratch_shapes=[
            pltpu.VMEM((count * chunks, LANES), F32),
            pltpu.VMEM((count, chunks * LANES), BF16),
            pltpu.VMEM((count, FF), BF16),
        ],
        compiler_params=pltpu.CompilerParams(vmem_limit_bytes=EXPERT_LIMIT),
        name="expert",
    )(x, up, down)


def combine_kernel(target_ref, gates_ref, hidden_ref, table_ref, out_ref, row_buf, *, topk):
    batch, width = hidden_ref.shape
    chunks = width // LANES
    for r in range(batch):
        total = jnp.zeros((chunks, LANES), F32)
        for k in range(topk):
            total += gates_ref[r, k] * table_ref[target_ref[r, k]].astype(F32)
        row_buf[r * chunks : (r + 1) * chunks, :] = total
    for j in range(chunks):
        cols = slice(j * LANES, (j + 1) * LANES)
        out_ref[:, cols] = (
            hidden_ref[:, cols] + row_buf[pl.ds(j, batch, stride=chunks), :]
        ).astype(BF16)


def combine(target, gates, hidden, table, topk):
    batch, width = hidden.shape
    smem = pl.BlockSpec(memory_space=pltpu.SMEM)
    vmem = pl.BlockSpec(memory_space=pltpu.VMEM)
    return pl.pallas_call(
        functools.partial(combine_kernel, topk=topk),
        out_shape=jax.ShapeDtypeStruct((batch, width), BF16),
        in_specs=[smem, smem, vmem, vmem],
        out_specs=vmem,
        scratch_shapes=[pltpu.VMEM((batch * width // LANES, LANES), F32)],
        compiler_params=pltpu.CompilerParams(vmem_limit_bytes=SMALL_LIMIT),
        name="combine",
    )(target, gates, hidden, table)


def per_device(
    residual_in,
    queries,
    latest_key_value,
    key_value_cache,
    cache_len,
    out_weight,
    norm_gain,
    router_weight,
    routes,
    expert_gate_up,
    expert_down,
):
    rows = queries.shape[0] * queries.shape[1]
    experts = router_weight.shape[1]
    topk = routes.shape[1]
    place = lax.axis_index("grp").reshape(1)
    own, other, coded = attend(
        place,
        cache_len,
        queries.reshape(rows, -1),
        latest_key_value.reshape((rows,) + latest_key_value.shape[2:]),
        routes.T,
        key_value_cache.reshape((rows,) + key_value_cache.shape[2:]),
        out_weight,
    )
    passed = lax.ppermute(other, "grp", [(0, 1), (1, 0)])
    base = residual_in.astype(F32) + own
    named, target = coded >> 1, coded ^ 1
    hidden, gates, slots = dispatch(
        target, named, base, passed, norm_gain.reshape(1, -1), router_weight, topk
    )
    block = (experts, CAP * slots.shape[1], LANES)
    received = lax.all_to_all(
        slots.reshape(block), ("grp", "dev"), split_axis=0, concat_axis=0, tiled=True
    )
    served = expert(received.reshape(slots.shape), expert_gate_up[0], expert_down[0])
    returned = lax.all_to_all(
        served.reshape(block), ("grp", "dev"), split_axis=0, concat_axis=0, tiled=True
    )
    return combine(target, gates, hidden, returned.reshape(slots.shape), topk)


def solution(mesh):
    placed = (
        P(("grp", "dev"), None),
        P(None, "dev", "grp"),
        P(None, "dev", "grp", None),
        P(None, "dev", "grp", None, None),
        P(None, "dev"),
        P("grp", None),
        P(),
        P(),
        P(("grp", "dev"), None),
        P(("grp", "dev"), None, None),
        P(("grp", "dev"), None, None),
    )
    return jax.shard_map(
        per_device, mesh=mesh, in_specs=placed, out_specs=P(("grp", "dev"), None), check_vma=False
    )
```

time: 79 us -> 68.6 us (0.87)
  Pallas kernels: 21.8 us -> 14.3 us
  local copies, waits for them, and re-layouts: 3.2 us -> 0.03 us
  other arithmetic: 0 us -> 1.62 us
  waiting for transfers between devices: 1.31 us -> 0.01 us
    pallas_call x1, Pallas kernels: 13 us -> 7.98 us  [attend(): pl.pallas_call(attend_kernel, out_shape=(half, half, jax.ShapeDtypeStruct...]
    pallas_call x1, Pallas kernels: 6.09 us -> 3.63 us  [expert(): pl.pallas_call(expert_kernel, out_shape=jax.ShapeDtypeStruct(x.shape, BF1...]
    unnamed x13 -> x10, local copies, waits for them, and re-layouts: 2.43 us -> 0.02 us
    ppermute x1, waiting for transfers between devices: 1.31 us -> 0.01 us  [per_device(): passed = lax.ppermute(other, 'grp', [(0, 1), (1, 0)])]
    add x0 -> x1, other arithmetic: none -> 0.92 us  [per_device(): base = residual_in.astype(F32) + own]
  transfers between devices with their start and end apart: 1 -> 1, of which waited for: 1 -> 0; matrix products, arithmetic and copies ran while one was open for 0% -> 2% of each run, Pallas kernels for 0% -> 0%
where the time goes in v3:
time: 68.6 us; the launch traced here: 68.4 us
  blocking collectives  52.3 us (76%)
  Pallas kernels  14.3 us (21%)
  other arithmetic  1.62 us (2%)
    all_to_all x1, blocking collectives, per_device(): lax.all_to_all(slots.reshape(block), ('grp', 'dev'), split_axis=0, concat...  29.2 us
    all_to_all x1, blocking collectives, per_device(): lax.all_to_all(served.reshape(block), ('grp', 'dev'), split_axis=0, conca...  23.2 us
    pallas_call x1, Pallas kernels, attend(): pl.pallas_call(attend_kernel, out_shape=(half, half, jax.ShapeDtypeStruct...  7.98 us
    pallas_call x1, Pallas kernels, expert(): pl.pallas_call(expert_kernel, out_shape=jax.ShapeDtypeStruct(x.shape, BF1...  3.63 us
    pallas_call x1, Pallas kernels, combine(): pl.pallas_call(functools.partial(combine_kernel, topk=topk), out_shape=ja...  1.59 us
  transfers between devices with their start and end apart: 1, of which 0 were waited for; matrix products, arithmetic and copies ran while one was open for 2% of the time, Pallas kernels for 0%

profile of v3, /device:TPU:0, one launch (start us, length us, event | category | flops | bytes accessed | tf_op | source)
XLA Modules:
  0.0 68.4 jit_solution(16988739494866622644)
XLA Ops:
  0.0 0.0 copy-start.4
  0.0 0.0 copy-start.3
  0.0 0.0 copy-start.2
  0.0 8.0 %attend.1 = (f32[16,2048]{1,0:T(8,128)}, f32[16,2048]{1,0:T(8,128)}, s32[16,128]{1,0:T(8,128)}) custom-call(s32[1]{0:T(128)} %bitcast.place_ref, s32[2,16]{1,0:T(2,128)} %length_hbm.1, bf16[32,2048]{1,0:T(8,128)(2,1)} %bitcast.18, bf16[32,2,256]{2,1,0:T(2,128)(2,1)} %bitcast.19, s32[8,16]{1,0:T(8,128)} %bitcast.20, bf16[32,2,256,256]{3,2,1,0:T(8,128)(2,1)} %bitcast.17, ...), custom_call_target="tpu_custom_call" | custom-call | tf_op jit(solution)/shard_map/attend/pallas_call | solution.py:200
  8.0 0.1 collective-permute-start
  8.1 0.0 copy-done.4
  8.1 0.0 copy-done.3
  8.1 0.9 %convert_add_fusion.base_ref = f32[16,2048]{1,0:T(8,128)S(1)} fusion(f32[16,2048]{1,0:T(8,128)} %get-tuple-element.12, bf16[16,2048]{1,0:T(8,128)(2,1)S(1)} %copy-done.3), kind=kLoop, calls=%fused_computation | loop fusion | flops 65536 | bytes 327680 | tf_op jit(solution)/shard_map/add | solution.py:391
  9.0 0.7 %broadcast_shift-right-arithmetic_fusion = (s32[16,128]{1,0:T(8,128)S(1)}, s32[16,128]{1,0:T(8,128)S(1)}) fusion(s32[16,128]{1,0:T(8,128)} %get-tuple-element.11), kind=kLoop, calls=%fused_computation.1 | loop fusion | flops 4096 | bytes 24576 | tf_op jit(solution)/shard_map/shift_right_arithmetic | solution.py:392
  9.7 0.0 collective-permute-done.passed_ref
  9.7 0.0 copy-done.2
  9.8 0.0 copy-start
  9.8 0.0 copy-start.1
  9.8 1.1 %dispatch.1 = (f32[16,2048]{1,0:T(8,128)S(1)}, f32[16,128]{1,0:T(8,128)S(1)}, bf16[256,16,128]{2,1,0:T(8,128)(2,1)S(1)}) custom-call(s32[16,128]{1,0:T(8,128)S(1)} %get-tuple-element.18.target_ref, s32[16,128]{1,0:T(8,128)S(1)} %get-tuple-element.17.named_ref, f32[16,2048]{1,0:T(8,128)S(1)} %convert_add_fusion.base_ref, ...), custom_call_target="tpu_custom_call" | custom-call | flops 10000000000 | bytes 3000000 | tf_op jit(solution)/shard_map/dispatch/pallas_call | solution.py:273
  10.9 29.2 %all_to_all.10 = bf16[128,32,128]{2,1,0:T(8,128)(2,1)S(1)} all-to-all(bf16[128,32,128]{2,1,0:T(8,128)(2,1)S(1)} %bitcast.16), channel_id=1, replica_groups=mesh['grp'=2,'dev'=64] {'grp','dev'}, dimensions={0} | all-to-all | bytes 2097152 | tf_op jit(solution)/shard_map/all_to_all | solution.py:397
  40.1 0.0 copy-done
  40.1 0.0 copy-done.1
  40.1 3.6 %expert.1 = bf16[256,16,128]{2,1,0:T(8,128)(2,1)S(1)} custom-call(bf16[256,16,128]{2,1,0:T(8,128)(2,1)S(1)} %bitcast.13, bf16[2048,1536]{1,0:T(8,128)(2,1)S(1)} %bitcast.11, bf16[768,2048]{1,0:T(8,128)(2,1)S(1)} %bitcast.15), custom_call_target="tpu_custom_call" | custom-call | tf_op jit(solution)/shard_map/expert/pallas_call | solution.py:319
  43.7 23.2 %all_to_all.11 = bf16[128,32,128]{2,1,0:T(8,128)(2,1)S(1)} all-to-all(bf16[128,32,128]{2,1,0:T(8,128)(2,1)S(1)} %bitcast.14), channel_id=1, replica_groups=mesh['grp'=2,'dev'=64] {'grp','dev'}, dimensions={0} | all-to-all | bytes 2097152 | tf_op jit(solution)/shard_map/all_to_all | solution.py:401
  66.9 1.6 %combine.1 = bf16[16,2048]{1,0:T(8,128)(2,1)} custom-call(s32[16,128]{1,0:T(8,128)S(1)} %get-tuple-element.18.target_ref, f32[16,128]{1,0:T(8,128)S(1)} %get-tuple-element.14.gates_ref, f32[16,2048]{1,0:T(8,128)S(1)} %get-tuple-element.15.hidden_ref, bf16[256,16,128]{2,1,0:T(8,128)(2,1)S(1)} %bitcast.12), custom_call_target="tpu_custom_call" | custom-call | tf_op jit(solution)/shard_map/combine/pallas_call | solution.py:353
  (1 shorter events, 0.0 us)
Async XLA Ops:
  0.0 8.1 %copy-start.4 = (bf16[2048]{0:T(1024)(128)(2,1)S(1)}, bf16[2048]{0:T(1024)(128)(2,1)}, u32[]{:S(2)}) copy-start(bf16[2048]{0:T(1024)(128)(2,1)} %param.17) | copy-start | bytes 12292
  0.0 8.1 %copy-start.3 = (bf16[16,2048]{1,0:T(8,128)(2,1)S(1)}, bf16[16,2048]{1,0:T(8,128)(2,1)}, u32[]{:S(2)}) copy-start(bf16[16,2048]{1,0:T(8,128)(2,1)} %param.11) | copy-start | bytes 196612
  0.0 9.7 %copy-start.2 = (bf16[2048,128]{1,0:T(8,128)(2,1)S(1)}, bf16[2048,128]{1,0:T(8,128)(2,1)}, u32[]{:S(2)}) copy-start(bf16[2048,128]{1,0:T(8,128)(2,1)} %router_ref.1) | copy-start | bytes 1572868
  8.0 1.8 %collective-permute-start = (f32[16,2048]{1,0:T(8,128)}, f32[16,2048]{1,0:T(8,128)S(1)}, u32[]{:S(2)}, u32[]{:S(2)}) collective-permute-start(f32[16,2048]{1,0:T(8,128)} %get-tuple-element.13), channel_id=1, source_target_pairs={{0,64},{64,0},{1,65},{65,1},{2,66},{66,2},{3,67},{67,3},{4,68},{68... | collective-permute-start | bytes 393224 | tf_op jit(solution)/shard_map/ppermute | solution.py:390
  9.8 30.3 %copy-start = (bf16[1,2048,1536]{2,1,0:T(8,128)(2,1)S(1)}, bf16[1,2048,1536]{2,1,0:T(8,128)(2,1)}, u32[]{:S(2)}) copy-start(bf16[1,2048,1536]{2,1,0:T(8,128)(2,1)} %param.20) | copy-start | bytes 18874372
  9.8 30.3 %copy-start.1 = (bf16[1,768,2048]{2,1,0:T(8,128)(2,1)S(1)}, bf16[1,768,2048]{2,1,0:T(8,128)(2,1)}, u32[]{:S(2)}) copy-start(bf16[1,768,2048]{2,1,0:T(8,128)(2,1)} %param.21) | copy-start | bytes 9437188

commit v4 on v3

--- a/solution.py
+++ b/solution.py
@@ -13,6 +13,9 @@
 FF = 768
 CAP = 2
 UNROLL = 8
+WHOLE = 8
+WSTEP = 0
+TSTEP = 0
 STEP = 256
 SPAN = 512
 W_CHUNKS = 4
@@ -39,7 +42,6 @@
     weight_hbm,
     own_ref,
     other_ref,
-    coded_ref,
     cache_buf,
     weight_buf,
     query_ref,
@@ -87,69 +89,60 @@
     ]
     for copy in small_copies:
         copy.start()
-    for row in range(UNROLL):
+    for row in range(WHOLE):
         whole_copy(row).start()
-    for row in range(UNROLL, rows):
+    for row in range(WHOLE, rows):
         cache_buf[row, :, :, HEAD_SIZE:] = jnp.zeros((kv_heads, positions, HEAD_SIZE), BF16)
     length_copy.wait()
-    for row in range(UNROLL, rows):
+    for row in range(WHOLE, rows):
         part_copy(row).start()
 
     for copy in small_copies:
         copy.wait()
-    topk, batch = routes_ref.shape
-    unit = lax.broadcasted_iota(jnp.int32, (topk, topk), 0) == lax.broadcasted_iota(
-        jnp.int32, (topk, topk), 1
-    )
-    routes = dot(
-        routes_ref[...].astype(BF16), jnp.where(unit, 1.0, 0.0).astype(BF16), ((0,), (0,))
-    ).astype(jnp.int32)
-    lane = lax.broadcasted_iota(jnp.int32, (batch, LANES), 1)
-    named = jnp.zeros((batch, LANES), F32)
-    for k in range(topk):
-        named += jnp.where(lane == routes[:, k : k + 1], 1.0, 0.0)
-    below = lax.broadcasted_iota(jnp.int32, (batch, batch), 0) > lax.broadcasted_iota(
-        jnp.int32, (batch, batch), 1
-    )
-    earlier = dot(jnp.where(below, 1.0, 0.0).astype(BF16), named.astype(BF16))
-    slot = lane.astype(F32) * CAP + earlier
-    target = jnp.zeros((batch, LANES), F32)
-    for k in range(topk):
-        found = jnp.sum(
-            jnp.where(lane == routes[:, k : k + 1], slot, 0.0), axis=1, keepdims=True
-        )
-        target = jnp.where(lane == k, found, target)
-    coded_ref[...] = target.astype(jnp.int32) ^ 1
-
     for j in range(q_heads):
         query_buf[pl.ds(j, rows, stride=q_heads), :] = query_ref[
             :, j * HEAD_SIZE : (j + 1) * HEAD_SIZE
         ].astype(F32)
     fresh_buf[...] = fresh_ref[...].astype(F32)
 
+    def place_rows():
+        topk, batch = routes_ref.shape
+        unit = lax.broadcasted_iota(jnp.int32, (topk, topk), 0) == lax.broadcasted_iota(
+            jnp.int32, (topk, topk), 1
+        )
+        routes = dot(
+            routes_ref[...].astype(BF16), jnp.where(unit, 1.0, 0.0).astype(BF16), ((0,), (0,))
+        ).astype(jnp.int32)
+        lane = lax.broadcasted_iota(jnp.int32, (batch, LANES), 1)
+        named = jnp.zeros((batch, LANES), F32)
+        for k in range(topk):
+            named += jnp.where(lane == routes[:, k : k + 1], 1.0, 0.0)
+        below = lax.broadcasted_iota(jnp.int32, (batch, batch), 0) > lax.broadcasted_iota(
+            jnp.int32, (batch, batch), 1
+        )
+        earlier = dot(jnp.where(below, 1.0, 0.0).astype(BF16), named.astype(BF16))
+        slot = lane.astype(F32) * CAP + earlier
+        target = jnp.zeros((batch, LANES), F32)
+        for k in range(topk):
+            found = jnp.sum(
+                jnp.where(lane == routes[:, k : k + 1], slot, 0.0), axis=1, keepdims=True
+            )
+            target = jnp.where(lane == k, found, target)
+        own_ref[batch:, :LANES] = target[: batch // 2]
+        own_ref[batch:, LANES : 2 * LANES] = target[batch // 2 :]
+        own_ref[batch:, 2 * LANES :] = jnp.zeros((batch // 2, width - 2 * LANES), F32)
+
     position = lax.broadcasted_iota(jnp.int32, (q_heads, positions), 1)
 
-    def some_rows(step, carry):
+    def score(step):
         first = step * UNROLL
-        base = pl.multiple_of(first * q_heads, UNROLL * q_heads)
-        query = query_buf[pl.ds(base, UNROLL * q_heads), :]
+        query = query_buf[first * q_heads : (first + UNROLL) * q_heads, :]
         query16 = query.astype(BF16)
-        @pl.when(step == 0)
-        def _():
-            for u in range(UNROLL):
-                whole_copy(u).wait()
-            for part in range(W_CHUNKS):
-                weight_copy(part).start()
-
-        @pl.when(step > 0)
-        def _():
-            for u in range(UNROLL):
-                part_copy(first + u).wait()
-
         scores, visible, new_key, new_value = [], [], [], []
         for u in range(UNROLL):
             fresh = fresh_buf[first + u]
-            visible.append(position < length_ref[(first + u) // half_rows, (first + u) % half_rows])
+            valid = length_ref[(first + u) // half_rows, (first + u) % half_rows]
+            visible.append(position < valid)
             for head in range(kv_heads):
                 begin = u * q_heads + head * group
                 keys = cache_buf[first + u, head, :, :HEAD_SIZE]
@@ -161,6 +154,10 @@
         new_key = jnp.concatenate(new_key, axis=0)
         own = jnp.exp(jnp.sum(query * new_key, axis=1, keepdims=True) * scale)
         raised = jnp.where(jnp.concatenate(visible, axis=0), jnp.exp(scores), 0.0)
+        return raised, own, jnp.concatenate(new_value, axis=0)
+
+    def mix(step, raised, own, new_value):
+        first = step * UNROLL
         total = jnp.sum(raised, axis=1, keepdims=True) + own
         weights = (raised / total).astype(BF16)
         own_weight = (own / total).astype(BF16).astype(F32)
@@ -170,11 +167,24 @@
                 begin = u * q_heads + head * group
                 values = cache_buf[first + u, head, :, HEAD_SIZE:]
                 mixed.append(dot(weights[begin : begin + group], values))
-        mixed = jnp.concatenate(mixed, axis=0) + own_weight * jnp.concatenate(new_value, axis=0)
-        mixed_buf[pl.ds(base, UNROLL * q_heads), :] = mixed
-        return carry
-
-    lax.fori_loop(0, rows // UNROLL, some_rows, 0)
+        mixed = jnp.concatenate(mixed, axis=0) + own_weight * new_value
+        mixed_buf[first * q_heads : (first + UNROLL) * q_heads, :] = mixed
+
+    ready = None
+    for step in range(rows // UNROLL):
+        for u in range(UNROLL):
+            row = step * UNROLL + u
+            (whole_copy if row < WHOLE else part_copy)(row).wait()
+        if step == WSTEP:
+            for part in range(W_CHUNKS):
+                weight_copy(part).start()
+        if step == TSTEP:
+            place_rows()
+        scored = score(step)
+        if step:
+            mix(step - 1, *ready)
+        ready = scored
+    mix(step, *ready)
 
     attended = jnp.concatenate(
         [mixed_buf[pl.ds(j, rows, stride=q_heads), :].astype(BF16) for j in range(q_heads)],
@@ -186,7 +196,7 @@
         cols = slice(part * span, (part + 1) * span)
         product = dot(attended, weight_buf[:, cols])
         top, bottom = product[: rows // 2], product[rows // 2 :]
-        own_ref[:, cols] = jnp.where(first_group, top, bottom)
+        own_ref[:half_rows, cols] = jnp.where(first_group, top, bottom)
         other_ref[:, cols] = jnp.where(first_group, bottom, top)
 
 
@@ -196,12 +206,15 @@
     smem = pl.BlockSpec(memory_space=pltpu.SMEM)
     vmem = pl.BlockSpec(memory_space=pltpu.VMEM)
     hbm = pl.BlockSpec(memory_space=pltpu.HBM)
-    half = jax.ShapeDtypeStruct((rows // 2, width), F32)
+    half = rows // 2
     return pl.pallas_call(
         attend_kernel,
-        out_shape=(half, half, jax.ShapeDtypeStruct((routes.shape[1], LANES), jnp.int32)),
+        out_shape=(
+            jax.ShapeDtypeStruct((half + half // 2, width), F32),
+            jax.ShapeDtypeStruct((half, width), F32),
+        ),
         in_specs=[smem, hbm, hbm, hbm, hbm, hbm, hbm],
-        out_specs=(vmem, vmem, vmem),
+        out_specs=(vmem, vmem),
         scratch_shapes=[
             pltpu.VMEM(cache.shape, BF16),
             pltpu.VMEM(weight.shape, BF16),
@@ -222,22 +235,29 @@
 
 
 def dispatch_kernel(
-    target_ref,
-    named_ref,
     base_ref,
     passed_ref,
     gain_ref,
     router_ref,
     hidden_ref,
+    target_ref,
     gates_ref,
     slots_ref,
     row_buf,
+    place_ref,
+    place_sem,
     *,
     topk,
 ):
-    batch, width = base_ref.shape
+    batch, width = passed_ref.shape
     chunks = width // LANES
-    hidden = base_ref[...] + passed_ref[...]
+    target = jnp.concatenate(
+        [base_ref[batch:, :LANES], base_ref[batch:, LANES : 2 * LANES]], axis=0
+    ).astype(jnp.int32)
+    target_ref[...] = target
+    place_copy = pltpu.make_async_copy(target_ref, place_ref, place_sem)
+    place_copy.start()
+    hidden = base_ref[:batch, :] + passed_ref[...]
     hidden_ref[...] = hidden
     meansq = jnp.mean(hidden * hidden, axis=1, keepdims=True)
     normed = (hidden * lax.rsqrt(meansq + 1e-06) * gain_ref[...].astype(F32)).astype(BF16)
@@ -247,7 +267,7 @@
         ].astype(F32)
 
     raised = jnp.exp(dot(normed, router_ref[...]))
-    routes = named_ref[...]
+    routes = target // CAP
     lane = lax.broadcasted_iota(jnp.int32, (batch, LANES), 1)
     total = jnp.zeros((batch, 1), F32)
     gates = jnp.zeros((batch, LANES), F32)
@@ -260,32 +280,37 @@
     gates_ref[...] = gates / total
 
     slots_ref[...] = jnp.zeros_like(slots_ref)
+    place_copy.wait()
     for r in range(batch):
         row = row_buf[r * chunks : (r + 1) * chunks, :].astype(BF16)
         for k in range(topk):
-            slots_ref[target_ref[r, k]] = row
-
-
-def dispatch(target, named, base, passed, gain, router, topk):
-    batch, width = base.shape
-    smem = pl.BlockSpec(memory_space=pltpu.SMEM)
+            slots_ref[place_ref[r, k]] = row
+
+
+def dispatch(base, passed, gain, router, topk):
+    batch, width = passed.shape
     vmem = pl.BlockSpec(memory_space=pltpu.VMEM)
     return pl.pallas_call(
         functools.partial(dispatch_kernel, topk=topk),
         out_shape=(
             jax.ShapeDtypeStruct((batch, width), F32),
+            jax.ShapeDtypeStruct((batch, LANES), jnp.int32),
             jax.ShapeDtypeStruct((batch, LANES), F32),
             jax.ShapeDtypeStruct((router.shape[1] * CAP, width // LANES, LANES), BF16),
         ),
-        in_specs=[smem] + [vmem] * 5,
-        out_specs=(vmem, vmem, vmem),
-        scratch_shapes=[pltpu.VMEM((batch * width // LANES, LANES), F32)],
+        in_specs=[vmem] * 4,
+        out_specs=(vmem, vmem, vmem, vmem),
+        scratch_shapes=[
+            pltpu.VMEM((batch * width // LANES, LANES), F32),
+            pltpu.SMEM((batch, LANES), jnp.int32),
+            pltpu.SemaphoreType.DMA,
+        ],
         compiler_params=pltpu.CompilerParams(vmem_limit_bytes=SMALL_LIMIT),
         cost_estimate=pl.CostEstimate(
             flops=10_000_000_000, bytes_accessed=3_000_000, transcendentals=0
         ),
         name="dispatch",
-    )(target, named, base, passed, gain, router)
+    )(base, passed, gain, router)
 
 
 def expert_kernel(x_ref, up_ref, down_ref, out_ref, wide, x_buf, act_buf):
@@ -378,7 +403,7 @@
     experts = router_weight.shape[1]
     topk = routes.shape[1]
     place = lax.axis_index("grp").reshape(1)
-    own, other, coded = attend(
+    own, other = attend(
         place,
         cache_len,
         queries.reshape(rows, -1),
@@ -388,10 +413,10 @@
         out_weight,
     )
     passed = lax.ppermute(other, "grp", [(0, 1), (1, 0)])
-    base = residual_in.astype(F32) + own
-    named, target = coded >> 1, coded ^ 1
-    hidden, gates, slots = dispatch(
-        target, named, base, passed, norm_gain.reshape(1, -1), router_weight, topk
+    below = own.shape[0] - residual_in.shape[0]
+    base = jnp.pad(residual_in.astype(F32), ((0, below), (0, 0))) + own
+    hidden, target, gates, slots = dispatch(
+        base, passed, norm_gain.reshape(1, -1), router_weight, topk
     )
     block = (experts, CAP * slots.shape[1], LANES)
     received = lax.all_to_all(

time: 68.6 us -> 67.5 us (0.984)
  Pallas kernels: 14.3 us -> 13.5 us
    shift_right_arithmetic x1 -> x0, other arithmetic: 0.7 us -> none  [per_device(): named, target = (coded >> 1, coded ^ 1)]
    pallas_call x1, Pallas kernels: 7.98 us -> 7.29 us  [attend(): pl.pallas_call(attend_kernel, out_shape=(jax.ShapeDtypeStruct((half + hal...]
  transfers between devices with their start and end apart: 1 -> 1, of which waited for: 0 -> 1; matrix products, arithmetic and copies ran while one was open for 2% -> 1% of each run, Pallas kernels for 0% -> 0%
where the time goes in v4:
time: 67.5 us; the launch traced here: 67.3 us
  blocking collectives  52.1 us (77%)
  Pallas kernels  13.5 us (20%)
  other arithmetic  0.95 us (1%)
    all_to_all x1, blocking collectives, per_device(): lax.all_to_all(slots.reshape(block), ('grp', 'dev'), split_axis=0, concat...  29 us
    all_to_all x1, blocking collectives, per_device(): lax.all_to_all(served.reshape(block), ('grp', 'dev'), split_axis=0, conca...  23.2 us
    pallas_call x1, Pallas kernels, attend(): pl.pallas_call(attend_kernel, out_shape=(jax.ShapeDtypeStruct((half + hal...  7.29 us
    pallas_call x1, Pallas kernels, expert(): pl.pallas_call(expert_kernel, out_shape=jax.ShapeDtypeStruct(x.shape, BF1...  3.62 us
    pallas_call x1, Pallas kernels, combine(): pl.pallas_call(functools.partial(combine_kernel, topk=topk), out_shape=ja...  1.59 us
  transfers between devices with their start and end apart: 1, of which 1 were waited for; matrix products, arithmetic and copies ran while one was open for 1% of the time, Pallas kernels for 0%

profile of v4, /device:TPU:0, one launch (start us, length us, event | category | flops | bytes accessed | tf_op | source)
XLA Modules:
  0.0 67.3 jit_solution(5298355235392022506)
XLA Ops:
  0.0 0.0 copy-start.2
  0.0 0.0 copy-start.3
  0.0 0.0 copy-start.1
  0.0 7.3 %attend.1 = (f32[24,2048]{1,0:T(8,128)}, f32[16,2048]{1,0:T(8,128)}) custom-call(s32[1]{0:T(128)} %bitcast.place_ref, s32[2,16]{1,0:T(2,128)} %length_hbm.1, bf16[32,2048]{1,0:T(8,128)(2,1)} %bitcast.20, bf16[32,2,256]{2,1,0:T(2,128)(2,1)} %bitcast.21, s32[8,16]{1,0:T(8,128)} %bitcast.22, bf16[32,2,256,256]{3,2,1,0:T(8,128)(2,1)} %bitcast.19, ...), custom_call_target="tpu_custom_call" | custom-call | tf_op jit(solution)/shard_map/attend/pallas_call | solution.py:210
  7.3 0.1 collective-permute-start
  7.4 0.0 copy-done.2
  7.4 0.9 %convert_add_fusion.base_ref = f32[24,2048]{1,0:T(8,128)S(1)} fusion(f32[24,2048]{1,0:T(8,128)} %get-tuple-element.11, bf16[16,2048]{1,0:T(8,128)(2,1)S(1)} %copy-done.2), kind=kLoop, calls=%fused_computation | loop fusion | flops 98304 | bytes 458752 | tf_op jit(solution)/shard_map/add | solution.py:417
  8.4 0.0 copy-done.3
  8.4 0.0 slice-start
  8.4 0.0 slice-start.1
  8.4 0.0 copy-start
  8.4 0.5 collective-permute-done.passed_ref
  8.9 0.0 copy-done.1
  8.9 1.0 %dispatch.1 = (f32[16,2048]{1,0:T(8,128)S(1)}, s32[16,128]{1,0:T(8,128)S(1)}, f32[16,128]{1,0:T(8,128)S(1)}, bf16[256,16,128]{2,1,0:T(8,128)(2,1)S(1)}) custom-call(f32[24,2048]{1,0:T(8,128)S(1)} %convert_add_fusion.base_ref, f32[16,2048]{1,0:T(8,128)S(1)} %collective-permute-done.passed_ref, bf16[1,2048]{1,0:T(2,128)(2,1)S(1)} %reshape.31.gain_ref, ...), custom_call_target="tpu_custom_call" | custom-call | flops 10000000000 | bytes 3000000 | tf_op jit(solution)/shard_map/dispatch/pallas_call | solution.py:293
  9.9 29.0 %all_to_all.10 = bf16[128,32,128]{2,1,0:T(8,128)(2,1)S(1)} all-to-all(bf16[128,32,128]{2,1,0:T(8,128)(2,1)S(1)} %bitcast.18), channel_id=1, replica_groups=mesh['grp'=2,'dev'=64] {'grp','dev'}, dimensions={0} | all-to-all | bytes 2097152 | tf_op jit(solution)/shard_map/all_to_all | solution.py:422
  38.9 0.0 slice-done
  38.9 0.0 slice-done.1
  38.9 0.0 copy-done
  38.9 3.6 %expert.1 = bf16[256,16,128]{2,1,0:T(8,128)(2,1)S(1)} custom-call(bf16[256,16,128]{2,1,0:T(8,128)(2,1)S(1)} %bitcast.15, bf16[2048,1536]{1,0:T(8,128)(2,1)S(1)} %bitcast.13, bf16[768,2048]{1,0:T(8,128)(2,1)S(1)} %bitcast.17), custom_call_target="tpu_custom_call" | custom-call | tf_op jit(solution)/shard_map/expert/pallas_call | solution.py:344
  42.5 23.2 %all_to_all.11 = bf16[128,32,128]{2,1,0:T(8,128)(2,1)S(1)} all-to-all(bf16[128,32,128]{2,1,0:T(8,128)(2,1)S(1)} %bitcast.16), channel_id=1, replica_groups=mesh['grp'=2,'dev'=64] {'grp','dev'}, dimensions={0} | all-to-all | bytes 2097152 | tf_op jit(solution)/shard_map/all_to_all | solution.py:426
  65.7 1.6 %combine.1 = bf16[16,2048]{1,0:T(8,128)(2,1)} custom-call(s32[16,128]{1,0:T(8,128)S(1)} %get-tuple-element.13.target_ref, f32[16,128]{1,0:T(8,128)S(1)} %get-tuple-element.14.gates_ref, f32[16,2048]{1,0:T(8,128)S(1)} %get-tuple-element.15.hidden_ref, bf16[256,16,128]{2,1,0:T(8,128)(2,1)S(1)} %bitcast.14), custom_call_target="tpu_custom_call" | custom-call | tf_op jit(solution)/shard_map/combine/pallas_call | solution.py:378
  (2 shorter events, 0.0 us)
Async XLA Ops:
  0.0 7.4 %copy-start.2 = (bf16[16,2048]{1,0:T(8,128)(2,1)S(1)}, bf16[16,2048]{1,0:T(8,128)(2,1)}, u32[]{:S(2)}) copy-start(bf16[16,2048]{1,0:T(8,128)(2,1)} %param.11) | copy-start | bytes 196612
  0.0 8.4 %copy-start.3 = (bf16[2048]{0:T(1024)(128)(2,1)S(1)}, bf16[2048]{0:T(1024)(128)(2,1)}, u32[]{:S(2)}) copy-start(bf16[2048]{0:T(1024)(128)(2,1)} %param.17) | copy-start | bytes 12292
  0.0 8.9 %copy-start.1 = (bf16[2048,128]{1,0:T(8,128)(2,1)S(1)}, bf16[2048,128]{1,0:T(8,128)(2,1)}, u32[]{:S(2)}) copy-start(bf16[2048,128]{1,0:T(8,128)(2,1)} %router_ref.1) | copy-start | bytes 1572868
  7.3 1.6 %collective-permute-start = (f32[16,2048]{1,0:T(8,128)}, f32[16,2048]{1,0:T(8,128)S(1)}, u32[]{:S(2)}, u32[]{:S(2)}) collective-permute-start(f32[16,2048]{1,0:T(8,128)} %get-tuple-element.12), channel_id=1, source_target_pairs={{0,64},{64,0},{1,65},{65,1},{2,66},{66,2},{3,67},{67,3},{4,68},{68... | collective-permute-start | bytes 393224 | tf_op jit(solution)/shard_map/ppermute | solution.py:415
  8.4 30.5 %slice-start = ((s8[6291456]{0:T(1024)(128)(4,1)}), s8[4194304]{0:T(1024)(128)(4,1)S(1)}, s32[]{:S(2)}) async-start(s8[6291456]{0:T(1024)(128)(4,1)} %bitcast.11), calls=%async_computation.2 | async-start | bytes 8388608
  8.4 30.5 %slice-start.1 = ((s8[6291456]{0:T(1024)(128)(4,1)}), s8[2097152]{0:T(1024)(128)(4,1)S(1)}, s32[]{:S(2)}) async-start(s8[6291456]{0:T(1024)(128)(4,1)} %bitcast.11), calls=%async_computation.3 | async-start | bytes 4194304
  8.4 30.5 %copy-start = (bf16[1,768,2048]{2,1,0:T(8,128)(2,1)S(1)}, bf16[1,768,2048]{2,1,0:T(8,128)(2,1)}, u32[]{:S(2)}) copy-start(bf16[1,768,2048]{2,1,0:T(8,128)(2,1)} %param.21) | copy-start | bytes 9437188

commit v5 on v4

--- a/solution.py
+++ b/solution.py
@@ -313,16 +313,12 @@
     )(base, passed, gain, router)
 
 
-def expert_kernel(x_ref, up_ref, down_ref, out_ref, wide, x_buf, act_buf):
+def expert_kernel(x_ref, up_ref, down_ref, out_ref, served_buf, x_buf, act_buf):
     count, chunks, _ = x_ref.shape
     width = chunks * LANES
     step = STEP
     span = SPAN
-    wide[...] = x_ref[...].reshape(count * chunks, LANES).astype(F32)
-    for j in range(chunks):
-        x_buf[:, j * LANES : (j + 1) * LANES] = wide[pl.ds(j, count, stride=chunks), :].astype(
-            BF16
-        )
+    x_buf[...] = x_ref[...].reshape(count, width)
     for part in range(FF // step):
         gate = dot(x_buf[...], up_ref[:, part * step : (part + 1) * step])
         lift = dot(x_buf[...], up_ref[:, FF + part * step : FF + (part + 1) * step])
@@ -331,11 +327,8 @@
         ).astype(BF16)
     for part in range(width // span):
         served = dot(act_buf[...], down_ref[:, part * span : (part + 1) * span])
-        for j in range(span // LANES):
-            wide[pl.ds(part * (span // LANES) + j, count, stride=chunks), :] = served[
-                :, j * LANES : (j + 1) * LANES
-            ]
-    out_ref[...] = wide[...].astype(BF16).reshape(count, chunks, LANES)
+        served_buf[:, part * span : (part + 1) * span] = served.astype(BF16)
+    out_ref[...] = served_buf[...].reshape(count, chunks, LANES)
 
 
 def expert(x, up, down):
@@ -347,7 +340,7 @@
         in_specs=[vmem, vmem, vmem],
         out_specs=vmem,
         scratch_shapes=[
-            pltpu.VMEM((count * chunks, LANES), F32),
+            pltpu.VMEM((count, chunks * LANES), BF16),
             pltpu.VMEM((count, chunks * LANES), BF16),
             pltpu.VMEM((count, FF), BF16),
         ],

time: 67.5 us -> 66.5 us (0.985)
  Pallas kernels: 13.5 us -> 12.4 us
    pallas_call x1, Pallas kernels: 3.62 us -> 2.62 us  [expert(): pl.pallas_call(expert_kernel, out_shape=jax.ShapeDtypeStruct(x.shape, BF1...]
where the time goes in v5:
time: 66.5 us; the launch traced here: 66.3 us
  blocking collectives  52.2 us (78%)
  Pallas kernels  12.4 us (19%)
  other arithmetic  0.95 us (1%)
    all_to_all x1, blocking collectives, per_device(): lax.all_to_all(slots.reshape(block), ('grp', 'dev'), split_axis=0, concat...  29.1 us
    all_to_all x1, blocking collectives, per_device(): lax.all_to_all(served.reshape(block), ('grp', 'dev'), split_axis=0, conca...  23.2 us
    pallas_call x1, Pallas kernels, attend(): pl.pallas_call(attend_kernel, out_shape=(jax.ShapeDtypeStruct((half + hal...  7.21 us
    pallas_call x1, Pallas kernels, expert(): pl.pallas_call(expert_kernel, out_shape=jax.ShapeDtypeStruct(x.shape, BF1...  2.62 us
    pallas_call x1, Pallas kernels, combine(): pl.pallas_call(functools.partial(combine_kernel, topk=topk), out_shape=ja...  1.59 us
  transfers between devices with their start and end apart: 1, of which 1 were waited for; matrix products, arithmetic and copies ran while one was open for 1% of the time, Pallas kernels for 0%

profile of v5, /device:TPU:0, one launch (start us, length us, event | category | flops | bytes accessed | tf_op | source)
XLA Modules:
  0.0 66.3 jit_solution(14990257903574403299)
XLA Ops:
  0.0 0.0 copy-start.2
  0.0 0.0 copy-start.3
  0.0 0.0 copy-start.1
  0.0 7.2 %attend.1 = (f32[24,2048]{1,0:T(8,128)}, f32[16,2048]{1,0:T(8,128)}) custom-call(s32[1]{0:T(128)} %bitcast.place_ref, s32[2,16]{1,0:T(2,128)} %length_hbm.1, bf16[32,2048]{1,0:T(8,128)(2,1)} %bitcast.20, bf16[32,2,256]{2,1,0:T(2,128)(2,1)} %bitcast.21, s32[8,16]{1,0:T(8,128)} %bitcast.22, bf16[32,2,256,256]{3,2,1,0:T(8,128)(2,1)} %bitcast.19, ...), custom_call_target="tpu_custom_call" | custom-call | tf_op jit(solution)/shard_map/attend/pallas_call | solution.py:210
  7.2 0.1 collective-permute-start
  7.3 0.0 copy-done.2
  7.3 0.9 %convert_add_fusion.base_ref = f32[24,2048]{1,0:T(8,128)S(1)} fusion(f32[24,2048]{1,0:T(8,128)} %get-tuple-element.11, bf16[16,2048]{1,0:T(8,128)(2,1)S(1)} %copy-done.2), kind=kLoop, calls=%fused_computation | loop fusion | flops 98304 | bytes 458752 | tf_op jit(solution)/shard_map/add | solution.py:410
  8.3 0.0 copy-done.3
  8.3 0.0 slice-start
  8.3 0.0 slice-start.1
  8.3 0.0 copy-start
  8.3 0.5 collective-permute-done.passed_ref
  8.9 0.0 copy-done.1
  8.9 1.0 %dispatch.1 = (f32[16,2048]{1,0:T(8,128)S(1)}, s32[16,128]{1,0:T(8,128)S(1)}, f32[16,128]{1,0:T(8,128)S(1)}, bf16[256,16,128]{2,1,0:T(8,128)(2,1)S(1)}) custom-call(f32[24,2048]{1,0:T(8,128)S(1)} %convert_add_fusion.base_ref, f32[16,2048]{1,0:T(8,128)S(1)} %collective-permute-done.passed_ref, bf16[1,2048]{1,0:T(2,128)(2,1)S(1)} %reshape.31.gain_ref, ...), custom_call_target="tpu_custom_call" | custom-call | flops 10000000000 | bytes 3000000 | tf_op jit(solution)/shard_map/dispatch/pallas_call | solution.py:293
  9.8 29.1 %all_to_all.10 = bf16[128,32,128]{2,1,0:T(8,128)(2,1)S(1)} all-to-all(bf16[128,32,128]{2,1,0:T(8,128)(2,1)S(1)} %bitcast.18), channel_id=1, replica_groups=mesh['grp'=2,'dev'=64] {'grp','dev'}, dimensions={0} | all-to-all | bytes 2097152 | tf_op jit(solution)/shard_map/all_to_all | solution.py:415
  38.9 0.0 slice-done
  38.9 0.0 slice-done.1
  38.9 0.0 copy-done
  38.9 2.6 %expert.1 = bf16[256,16,128]{2,1,0:T(8,128)(2,1)S(1)} custom-call(bf16[256,16,128]{2,1,0:T(8,128)(2,1)S(1)} %bitcast.15, bf16[2048,1536]{1,0:T(8,128)(2,1)S(1)} %bitcast.13, bf16[768,2048]{1,0:T(8,128)(2,1)S(1)} %bitcast.17), custom_call_target="tpu_custom_call" | custom-call | tf_op jit(solution)/shard_map/expert/pallas_call | solution.py:337
  41.5 23.2 %all_to_all.11 = bf16[128,32,128]{2,1,0:T(8,128)(2,1)S(1)} all-to-all(bf16[128,32,128]{2,1,0:T(8,128)(2,1)S(1)} %bitcast.16), channel_id=1, replica_groups=mesh['grp'=2,'dev'=64] {'grp','dev'}, dimensions={0} | all-to-all | bytes 2097152 | tf_op jit(solution)/shard_map/all_to_all | solution.py:419
  64.7 1.6 %combine.1 = bf16[16,2048]{1,0:T(8,128)(2,1)} custom-call(s32[16,128]{1,0:T(8,128)S(1)} %get-tuple-element.13.target_ref, f32[16,128]{1,0:T(8,128)S(1)} %get-tuple-element.14.gates_ref, f32[16,2048]{1,0:T(8,128)S(1)} %get-tuple-element.15.hidden_ref, bf16[256,16,128]{2,1,0:T(8,128)(2,1)S(1)} %bitcast.14), custom_call_target="tpu_custom_call" | custom-call | tf_op jit(solution)/shard_map/combine/pallas_call | solution.py:371
  (2 shorter events, 0.0 us)
Async XLA Ops:
  0.0 7.3 %copy-start.2 = (bf16[16,2048]{1,0:T(8,128)(2,1)S(1)}, bf16[16,2048]{1,0:T(8,128)(2,1)}, u32[]{:S(2)}) copy-start(bf16[16,2048]{1,0:T(8,128)(2,1)} %param.11) | copy-start | bytes 196612
  0.0 8.3 %copy-start.3 = (bf16[2048]{0:T(1024)(128)(2,1)S(1)}, bf16[2048]{0:T(1024)(128)(2,1)}, u32[]{:S(2)}) copy-start(bf16[2048]{0:T(1024)(128)(2,1)} %param.17) | copy-start | bytes 12292
  0.0 8.9 %copy-start.1 = (bf16[2048,128]{1,0:T(8,128)(2,1)S(1)}, bf16[2048,128]{1,0:T(8,128)(2,1)}, u32[]{:S(2)}) copy-start(bf16[2048,128]{1,0:T(8,128)(2,1)} %router_ref.1) | copy-start | bytes 1572868
  7.2 1.6 %collective-permute-start = (f32[16,2048]{1,0:T(8,128)}, f32[16,2048]{1,0:T(8,128)S(1)}, u32[]{:S(2)}, u32[]{:S(2)}) collective-permute-start(f32[16,2048]{1,0:T(8,128)} %get-tuple-element.12), channel_id=1, source_target_pairs={{0,64},{64,0},{1,65},{65,1},{2,66},{66,2},{3,67},{67,3},{4,68},{68... | collective-permute-start | bytes 393224 | tf_op jit(solution)/shard_map/ppermute | solution.py:408
  8.3 30.6 %slice-start = ((s8[6291456]{0:T(1024)(128)(4,1)}), s8[4194304]{0:T(1024)(128)(4,1)S(1)}, s32[]{:S(2)}) async-start(s8[6291456]{0:T(1024)(128)(4,1)} %bitcast.11), calls=%async_computation.2 | async-start | bytes 8388608
  8.3 30.6 %slice-start.1 = ((s8[6291456]{0:T(1024)(128)(4,1)}), s8[2097152]{0:T(1024)(128)(4,1)S(1)}, s32[]{:S(2)}) async-start(s8[6291456]{0:T(1024)(128)(4,1)} %bitcast.11), calls=%async_computation.3 | async-start | bytes 4194304
  8.3 30.6 %copy-start = (bf16[1,768,2048]{2,1,0:T(8,128)(2,1)S(1)}, bf16[1,768,2048]{2,1,0:T(8,128)(2,1)}, u32[]{:S(2)}) copy-start(bf16[1,768,2048]{2,1,0:T(8,128)(2,1)} %param.21) | copy-start | bytes 9437188

commit v6 on v5

--- a/solution.py
+++ b/solution.py
@@ -186,10 +186,7 @@
         ready = scored
     mix(step, *ready)
 
-    attended = jnp.concatenate(
-        [mixed_buf[pl.ds(j, rows, stride=q_heads), :].astype(BF16) for j in range(q_heads)],
-        axis=1,
-    )
+    attended = mixed_buf[...].astype(BF16).reshape(rows, q_heads * HEAD_SIZE)
     first_group = place_ref[0] == 0
     for part in range(W_CHUNKS):
         weight_copy(part).wait()
@@ -261,10 +258,7 @@
     hidden_ref[...] = hidden
     meansq = jnp.mean(hidden * hidden, axis=1, keepdims=True)
     normed = (hidden * lax.rsqrt(meansq + 1e-06) * gain_ref[...].astype(F32)).astype(BF16)
-    for j in range(chunks):
-        row_buf[pl.ds(j, batch, stride=chunks), :] = normed[
-            :, j * LANES : (j + 1) * LANES
-        ].astype(F32)
+    row_buf[...] = normed.reshape(batch, chunks, LANES)
 
     raised = jnp.exp(dot(normed, router_ref[...]))
     routes = target // CAP
@@ -282,7 +276,7 @@
     slots_ref[...] = jnp.zeros_like(slots_ref)
     place_copy.wait()
     for r in range(batch):
-        row = row_buf[r * chunks : (r + 1) * chunks, :].astype(BF16)
+        row = row_buf[r]
         for k in range(topk):
             slots_ref[place_ref[r, k]] = row
 
@@ -301,7 +295,7 @@
         in_specs=[vmem] * 4,
         out_specs=(vmem, vmem, vmem, vmem),
         scratch_shapes=[
-            pltpu.VMEM((batch * width // LANES, LANES), F32),
+            pltpu.VMEM((batch, width // LANES, LANES), BF16),
             pltpu.SMEM((batch, LANES), jnp.int32),
             pltpu.SemaphoreType.DMA,
         ],

time: 66.5 us -> 66.5 us (level)
  no operation moved by 1% of the time
where the time goes in v6:
time: 66.5 us; the launch traced here: 66.3 us
  blocking collectives  52.3 us (79%)
  Pallas kernels  12.3 us (18%)
  other arithmetic  0.95 us (1%)
    all_to_all x1, blocking collectives, per_device(): lax.all_to_all(slots.reshape(block), ('grp', 'dev'), split_axis=0, concat...  29.1 us
    all_to_all x1, blocking collectives, per_device(): lax.all_to_all(served.reshape(block), ('grp', 'dev'), split_axis=0, conca...  23.2 us
    pallas_call x1, Pallas kernels, attend(): pl.pallas_call(attend_kernel, out_shape=(jax.ShapeDtypeStruct((half + hal...  7.15 us
    pallas_call x1, Pallas kernels, expert(): pl.pallas_call(expert_kernel, out_shape=jax.ShapeDtypeStruct(x.shape, BF1...  2.62 us
    pallas_call x1, Pallas kernels, combine(): pl.pallas_call(functools.partial(combine_kernel, topk=topk), out_shape=ja...  1.59 us
  transfers between devices with their start and end apart: 1, of which 1 were waited for; matrix products, arithmetic and copies ran while one was open for 1% of the time, Pallas kernels for 0%

profile of v6, /device:TPU:0, one launch (start us, length us, event | category | flops | bytes accessed | tf_op | source)
XLA Modules:
  0.0 66.3 jit_solution(11699838971787251304)
XLA Ops:
  0.0 0.0 copy-start.2
  0.0 0.0 copy-start.3
  0.0 0.0 copy-start.1
  0.0 7.2 %attend.1 = (f32[24,2048]{1,0:T(8,128)}, f32[16,2048]{1,0:T(8,128)}) custom-call(s32[1]{0:T(128)} %bitcast.place_ref, s32[2,16]{1,0:T(2,128)} %length_hbm.1, bf16[32,2048]{1,0:T(8,128)(2,1)} %bitcast.20, bf16[32,2,256]{2,1,0:T(2,128)(2,1)} %bitcast.21, s32[8,16]{1,0:T(8,128)} %bitcast.22, bf16[32,2,256,256]{3,2,1,0:T(8,128)(2,1)} %bitcast.19, ...), custom_call_target="tpu_custom_call" | custom-call | tf_op jit(solution)/shard_map/attend/pallas_call | solution.py:207
  7.2 0.1 collective-permute-start
  7.3 0.0 copy-done.2
  7.3 0.9 %convert_add_fusion.base_ref = f32[24,2048]{1,0:T(8,128)S(1)} fusion(f32[24,2048]{1,0:T(8,128)} %get-tuple-element.11, bf16[16,2048]{1,0:T(8,128)(2,1)S(1)} %copy-done.2), kind=kLoop, calls=%fused_computation | loop fusion | flops 98304 | bytes 458752 | tf_op jit(solution)/shard_map/add | solution.py:404
  8.2 0.0 copy-done.3
  8.2 0.0 slice-start
  8.3 0.0 slice-start.1
  8.3 0.0 copy-start
  8.3 0.5 collective-permute-done.passed_ref
  8.8 0.0 copy-done.1
  8.8 1.0 %dispatch.1 = (f32[16,2048]{1,0:T(8,128)S(1)}, s32[16,128]{1,0:T(8,128)S(1)}, f32[16,128]{1,0:T(8,128)S(1)}, bf16[256,16,128]{2,1,0:T(8,128)(2,1)S(1)}) custom-call(f32[24,2048]{1,0:T(8,128)S(1)} %convert_add_fusion.base_ref, f32[16,2048]{1,0:T(8,128)S(1)} %collective-permute-done.passed_ref, bf16[1,2048]{1,0:T(2,128)(2,1)S(1)} %reshape.31.gain_ref, ...), custom_call_target="tpu_custom_call" | custom-call | flops 10000000000 | bytes 3000000 | tf_op jit(solution)/shard_map/dispatch/pallas_call | solution.py:287
  9.8 29.1 %all_to_all.10 = bf16[128,32,128]{2,1,0:T(8,128)(2,1)S(1)} all-to-all(bf16[128,32,128]{2,1,0:T(8,128)(2,1)S(1)} %bitcast.18), channel_id=1, replica_groups=mesh['grp'=2,'dev'=64] {'grp','dev'}, dimensions={0} | all-to-all | bytes 2097152 | tf_op jit(solution)/shard_map/all_to_all | solution.py:409
  38.9 0.0 slice-done
  38.9 0.0 slice-done.1
  38.9 0.0 copy-done
  38.9 2.6 %expert.1 = bf16[256,16,128]{2,1,0:T(8,128)(2,1)S(1)} custom-call(bf16[256,16,128]{2,1,0:T(8,128)(2,1)S(1)} %bitcast.15, bf16[2048,1536]{1,0:T(8,128)(2,1)S(1)} %bitcast.13, bf16[768,2048]{1,0:T(8,128)(2,1)S(1)} %bitcast.17), custom_call_target="tpu_custom_call" | custom-call | tf_op jit(solution)/shard_map/expert/pallas_call | solution.py:331
  41.6 23.2 %all_to_all.11 = bf16[128,32,128]{2,1,0:T(8,128)(2,1)S(1)} all-to-all(bf16[128,32,128]{2,1,0:T(8,128)(2,1)S(1)} %bitcast.16), channel_id=1, replica_groups=mesh['grp'=2,'dev'=64] {'grp','dev'}, dimensions={0} | all-to-all | bytes 2097152 | tf_op jit(solution)/shard_map/all_to_all | solution.py:413
  64.7 1.6 %combine.1 = bf16[16,2048]{1,0:T(8,128)(2,1)} custom-call(s32[16,128]{1,0:T(8,128)S(1)} %get-tuple-element.13.target_ref, f32[16,128]{1,0:T(8,128)S(1)} %get-tuple-element.14.gates_ref, f32[16,2048]{1,0:T(8,128)S(1)} %get-tuple-element.15.hidden_ref, bf16[256,16,128]{2,1,0:T(8,128)(2,1)S(1)} %bitcast.14), custom_call_target="tpu_custom_call" | custom-call | tf_op jit(solution)/shard_map/combine/pallas_call | solution.py:365
  (2 shorter events, 0.0 us)
Async XLA Ops:
  0.0 7.3 %copy-start.2 = (bf16[16,2048]{1,0:T(8,128)(2,1)S(1)}, bf16[16,2048]{1,0:T(8,128)(2,1)}, u32[]{:S(2)}) copy-start(bf16[16,2048]{1,0:T(8,128)(2,1)} %param.11) | copy-start | bytes 196612
  0.0 8.2 %copy-start.3 = (bf16[2048]{0:T(1024)(128)(2,1)S(1)}, bf16[2048]{0:T(1024)(128)(2,1)}, u32[]{:S(2)}) copy-start(bf16[2048]{0:T(1024)(128)(2,1)} %param.17) | copy-start | bytes 12292
  0.0 8.8 %copy-start.1 = (bf16[2048,128]{1,0:T(8,128)(2,1)S(1)}, bf16[2048,128]{1,0:T(8,128)(2,1)}, u32[]{:S(2)}) copy-start(bf16[2048,128]{1,0:T(8,128)(2,1)} %router_ref.1) | copy-start | bytes 1572868
  7.2 1.6 %collective-permute-start = (f32[16,2048]{1,0:T(8,128)}, f32[16,2048]{1,0:T(8,128)S(1)}, u32[]{:S(2)}, u32[]{:S(2)}) collective-permute-start(f32[16,2048]{1,0:T(8,128)} %get-tuple-element.12), channel_id=1, source_target_pairs={{0,64},{64,0},{1,65},{65,1},{2,66},{66,2},{3,67},{67,3},{4,68},{68... | collective-permute-start | bytes 393224 | tf_op jit(solution)/shard_map/ppermute | solution.py:402
  8.2 30.7 %slice-start = ((s8[6291456]{0:T(1024)(128)(4,1)}), s8[4194304]{0:T(1024)(128)(4,1)S(1)}, s32[]{:S(2)}) async-start(s8[6291456]{0:T(1024)(128)(4,1)} %bitcast.11), calls=%async_computation.2 | async-start | bytes 8388608
  8.3 30.7 %slice-start.1 = ((s8[6291456]{0:T(1024)(128)(4,1)}), s8[2097152]{0:T(1024)(128)(4,1)S(1)}, s32[]{:S(2)}) async-start(s8[6291456]{0:T(1024)(128)(4,1)} %bitcast.11), calls=%async_computation.3 | async-start | bytes 4194304
  8.3 30.7 %copy-start = (bf16[1,768,2048]{2,1,0:T(8,128)(2,1)S(1)}, bf16[1,768,2048]{2,1,0:T(8,128)(2,1)}, u32[]{:S(2)}) copy-start(bf16[1,768,2048]{2,1,0:T(8,128)(2,1)} %param.21) | copy-start | bytes 9437188
